TPU v7x, 256 devices: a whole 4x4x8 slice. The times are simulated.
256 devices in a mesh: dp: 32 (over z_lo, x, core), fac: 8 (over z_hi, y).
Axes of the slice: x: 4, y: 4, z: 8 (z_hi: 2, z_lo: 4; z = z_hi * 4 + z_lo), core: 2. Of those that a mesh axis runs over, the one named last changes fastest.
Arguments:
- occupations: int32 [64, 256], P('dp'), may hold values from 0 to 1, as said below
- stream: bfloat16 [16384, 2048], P('dp', 'fac'), may hold values from -6 to 6
- norm_gain: float32 [2048], replicated, may hold values from 0.1 to 1.9
- probs: bfloat16 [64, 16, 256, 256], P('dp', 'fac'), may hold values from 0 to 1, as said below
- w_out: bfloat16 [2048, 2048], P('fac', 'dp'), may hold values from -0.125 to 0.125
- cotangent: bfloat16 [16384, 2048], P('dp', 'fac'), may hold values from -6 to 6
Outputs:
- update: float32 [2048, 2048], P('dp', 'fac')
Inputs may be any that keep to these rules, and one draw needn't show every extreme that they name: `occupations`: each sample holds exactly 48 ones. `probs`: within each sample and head, entries with the key after the query are zero and each row sums to one up to bfloat16 rounding.
All inputs are finite; a program needn't handle non-finite values.
Results may differ from a plain program's by a relative error of at most 0.0051.
Values may be sent and summed in bfloat16 or wider, within the bound.
A program may use at most 64 MiB of HBM per device.

v0:
```python
import jax
import jax.numpy as jnp
from jax import lax
from jax.sharding import PartitionSpec as P

ORBS = 256
NE = 48


damping = 0.1
epsilon = 1e-06
highest = lax.Precision.HIGHEST
contract_first = (((0,), (0,)), ((), ()))


def keep_mask(occupations):
    before = jnp.cumsum(occupations, axis=1) - occupations
    position = lax.broadcasted_iota(jnp.int32, occupations.shape, 1)
    forced = (before == NE) | (position - before == ORBS - NE)
    return 1 - forced.astype(jnp.int32)


def panel_rows(block):
    return lax.all_gather(block, "fac", axis=2, tiled=True)


def panel_product(left_rows, right_block):
    return jnp.einsum(
        "brk,bkc->brc",
        left_rows,
        lax.all_gather(right_block, "dp", axis=1, tiled=True),
        precision=highest,
    )


def per_device(occupations, stream, norm_gain, probs, w_out, cotangent):
    width = norm_gain.shape[0]
    samples = occupations.shape[0]
    tokens = samples * ORBS
    data_count = lax.axis_size("dp")
    fac_count = lax.axis_size("fac")
    block_rows = width // data_count
    block_cols = width // fac_count
    data_index = lax.axis_index("dp")
    fac_index = lax.axis_index("fac")
    scale = 1.0 / (tokens * data_count)
    stream_whole, cotangent_whole = (
        lax.all_gather(stream, "fac", axis=1, tiled=True),
        lax.all_gather(cotangent, "fac", axis=1, tiled=True),
    )
    values = stream_whole.astype(jnp.float32)
    mean_square = jnp.mean(values * values, axis=1, keepdims=True)
    normed = (values * lax.rsqrt(mean_square + epsilon) * norm_gain).astype(jnp.bfloat16)
    normed_cols = lax.dynamic_slice_in_dim(normed, fac_index * block_cols, block_cols, 1)
    keep = keep_mask(occupations).reshape(tokens, 1).astype(jnp.bfloat16)
    upstream = cotangent_whole * keep
    out_grad = lax.dot_general(
        upstream,
        lax.all_gather(w_out, "dp", axis=1, tiled=True),
        (((1,), (1,)), ((), ())),
        preferred_element_type=jnp.float32,
    ).astype(jnp.bfloat16)
    local_heads = probs.shape[1]
    head_width = block_cols // local_heads
    per_head = out_grad.reshape(samples, ORBS, local_heads, head_width)
    value_local = jnp.einsum("shij,sihe->sjhe", probs, per_head, preferred_element_type=jnp.float32)
    value_local = value_local.reshape(tokens, block_cols).astype(jnp.bfloat16)
    value_whole = lax.all_gather(value_local, "fac", axis=1, tiled=True)
    g_part = (
        lax.dot_general(
            value_whole, value_local, contract_first, preferred_element_type=jnp.float32
        )
        * scale
    )
    grad_part = (
        lax.dot_general(normed, value_local, contract_first, preferred_element_type=jnp.float32)
        * scale
    )
    a_part = (
        lax.dot_general(normed, normed_cols, contract_first, preferred_element_type=jnp.float32)
        * scale
    )
    a_block, g_block, grad_block = (
        lax.psum_scatter(a_part, "dp", scatter_dimension=0, tiled=True),
        lax.psum_scatter(g_part, "dp", scatter_dimension=0, tiled=True),
        lax.psum_scatter(grad_part, "dp", scatter_dimension=0, tiled=True),
    )
    row_ids = data_index * block_rows + lax.broadcasted_iota(jnp.int32, (block_rows, block_cols), 0)
    col_ids = fac_index * block_cols + lax.broadcasted_iota(jnp.int32, (block_rows, block_cols), 1)
    identity_block = (row_ids == col_ids).astype(jnp.float32)
    a_block = a_block + damping * identity_block
    g_block = g_block + damping * identity_block
    norm_a, norm_g = lax.psum(
        (jnp.sum(a_block * a_block), jnp.sum(g_block * g_block)), ("dp", "fac")
    )
    alphas = (1.0 / jnp.sqrt(jnp.stack([norm_a, norm_g]))).reshape(2, 1, 1)
    factors = jnp.stack([a_block, g_block])
    iterate = 2.0 * alphas * identity_block[None] - alphas * alphas * factors
    product = panel_product(panel_rows(factors), iterate)
    iterate = 2.0 * iterate - panel_product(panel_rows(iterate), product)
    left_side = panel_product(panel_rows(iterate[0:1]), grad_block[None])
    pre = panel_product(panel_rows(left_side), iterate[1:2])[0]
    inner_sum = lax.psum(jnp.sum(grad_block * pre), ("dp", "fac"))
    return pre * (width / jnp.sqrt(inner_sum + epsilon))


def solution(mesh):
    placed = (
        P("dp", None),
        P("dp", "fac"),
        P(),
        P("dp", "fac", None, None),
        P("fac", "dp"),
        P("dp", "fac"),
    )
    return jax.shard_map(
        per_device, mesh=mesh, in_specs=placed, out_specs=P("dp", "fac"), check_vma=False
    )
```

profile of v0, /device:TPU:1, one launch (start us, length us, event | category | flops | bytes accessed | tf_op | source)
XLA Modules:
  0.0 1268.2 jit_solution(9189900301036835949)
XLA Ops:
  6.5 0.7 all-gather.17.cloned.1.call-update
  7.3 0.7 all-gather.15.cloned.1.call-update
  8.1 0.7 all-gather.13.cloned.1.call-update
  8.8 0.7 reshape.106
  9.5 0.6 reduce-window.6
  10.1 0.2 slice_reduce_fusion
  10.3 0.2 reduce-window.9
  10.5 0.1 add_bitcast_fusion
  10.6 0.7 fusion.20
  11.3 61.1 %all-gather.17.cloned.1.call-done = bf16[256,2048]{0,1:T(8,128)(2,1)} async-done(((bf16[256,64]{0,1:T(8,128)(2,1)}), bf16[256,2048]{0,1:T(8,128)(2,1)}) %all-gather.17.cloned.1.call-update) | async-done | bytes 1048592 | tf_op jit(solution)/shard_map/all_gather | solution.py:59
  72.4 76.7 %all-gather.15.cloned.1.call-done = bf16[512,2048]{1,0:T(8,128)(2,1)} async-done(((bf16[512,256]{1,0:T(8,128)(2,1)}), bf16[512,2048]{1,0:T(8,128)(2,1)}) %all-gather.15.cloned.1.call-update) | async-done | bytes 2097168 | tf_op jit(solution)/shard_map/all_gather | solution.py:49
  149.1 2.6 fusion.7
  151.7 0.1 reshape.108
  151.8 0.3 fusion.10
  152.1 0.2 copy.9
  152.3 0.7 copy.25
  153.1 71.3 %all-gather.13.cloned.1.call-done = bf16[512,2048]{1,0:T(8,128)(2,1)} async-done(((bf16[512,256]{1,0:T(8,128)(2,1)}), bf16[512,2048]{1,0:T(8,128)(2,1)}) %all-gather.13.cloned.1.call-update) | async-done | bytes 2097168 | tf_op jit(solution)/shard_map/all_gather | solution.py:48
  224.4 2.2 fusion
  226.7 0.5 fusion.2
  227.2 2.1 convolution_multiply_fusion.2
  229.4 70.2 %all-gather.19.cloned.1.call-done = bf16[512,2048]{1,0:T(8,128)(2,1)} async-done(((bf16[512,256]{1,0:T(8,128)(2,1)}), bf16[512,2048]{1,0:T(8,128)(2,1)}) %all-gather.19.cloned.1.call-update) | async-done | bytes 2097168 | tf_op jit(solution)/shard_map/all_gather | solution.py:68
  299.6 3.7 convolution_multiply_fusion.1
  303.4 0.1 compare_convert_fusion
  303.5 136.7 %reduce-scatter.4.cloned.1.call-done = f32[64,256]{1,0:T(8,128)} async-done(((f32[2048,256]{1,0:T(8,128)}), f32[64,256]{1,0:T(8,128)}) %reduce-scatter.4.cloned.1.call-update) | async-done | bytes 65552 | tf_op jit(solution)/shard_map/reduce_scatter | solution.py:84
  440.2 145.6 %reduce-scatter.6.cloned.1.call-done = f32[64,256]{1,0:T(8,128)} async-done(((f32[2048,256]{1,0:T(8,128)}), f32[64,256]{1,0:T(8,128)}) %reduce-scatter.6.cloned.1.call-update) | async-done | bytes 65552 | tf_op jit(solution)/shard_map/reduce_scatter | solution.py:85
  585.8 1.6 multiply_reduce_fusion.2
  587.4 81.2 %all-reduce = (f32[1]{0:T(128)}, f32[1]{0:T(128)}) all-reduce(f32[1]{0:T(128)} %bitcast.2, f32[1]{0:T(128)} %bitcast), channel_id=1, replica_groups=mesh['dp'=32,'fac'=8] {'dp','fac'}, use_global_device_ids=true, to_apply=%region_8.9 | all-reduce | flops 2 | bytes 16 | tf_op jit(solution)/shard_map/psum | solution.py:93
  668.6 1.4 broadcast_multiply_fusion.1
  670.0 0.7 pad_maximum_fusion
  670.8 0.7 all-gather.25.cloned.1.call-update
  671.5 2.1 convolution_multiply_fusion
  673.7 0.5 all-gather.21.cloned.1.call-update
  674.3 51.4 %all-gather.23.cloned.1.call-done = f32[2,64,2048]{2,1,0:T(8,128)} async-done(((f32[2,64,256]{2,1,0:T(8,128)}), f32[2,64,2048]{2,1,0:T(8,128)}) %all-gather.23.cloned.1.call-update) | async-done | bytes 1048592 | tf_op jit(solution)/shard_map/all_gather | solution.py:24
  725.6 62.3 %all-gather.25.cloned.1.call-done = f32[2,2048,256]{2,1,0:T(8,128)} async-done(((f32[2,64,256]{2,1,0:T(8,128)}), f32[2,2048,256]{2,1,0:T(8,128)}) %all-gather.25.cloned.1.call-update) | async-done | bytes 4194320 | tf_op jit(solution)/shard_map/all_gather | solution.py:31
  788.0 5.8 fusion.24
  793.9 136.6 %reduce-scatter.8.cloned.1.call-done = f32[64,256]{1,0:T(8,128)} async-done(((f32[2048,256]{1,0:T(8,128)}), f32[64,256]{1,0:T(8,128)}) %reduce-scatter.8.cloned.1.call-update) | async-done | bytes 65552 | tf_op jit(solution)/shard_map/reduce_scatter | solution.py:86
  930.6 64.4 %all-gather.21.cloned.1.call-done = f32[2,64,2048]{2,1,0:T(8,128)} async-done(((f32[2,64,256]{2,1,0:T(8,128)}), f32[2,64,2048]{2,1,0:T(8,128)}) %all-gather.21.cloned.1.call-update) | async-done | bytes 1048592 | tf_op jit(solution)/shard_map/all_gather | solution.py:24
  995.0 62.5 %all-gather.27.cloned.1.call-done = f32[2,2048,256]{2,1,0:T(8,128)} async-done(((f32[2,64,256]{2,1,0:T(8,128)}), f32[2,2048,256]{2,1,0:T(8,128)}) %all-gather.27.cloned.1.call-update) | async-done | bytes 4194320 | tf_op jit(solution)/shard_map/all_gather | solution.py:31
  1057.5 5.2 convolution_subtract_fusion
  1062.7 0.6 fusion.23
  1063.3 39.8 %all_gather.44 = f32[1,64,2048]{2,1,0:T(8,128)S(1)} all-gather(f32[1,64,256]{2,1,0:T(8,128)S(1)} %get-tuple-element.10), channel_id=1, replica_groups=mesh['dp'=32,'fac'=8] {'fac'}, dimensions={2}, use_global_device_ids=true | all-gather | bytes 589824 | tf_op jit(solution)/shard_map/all_gather | solution.py:24
  1103.2 16.6 %all-gather.31.cloned.1.call-done = f32[2048,256]{1,0:T(8,128)} async-done(((f32[64,256]{1,0:T(8,128)}), f32[2048,256]{1,0:T(8,128)}) %all-gather.31.cloned.1.call-update) | async-done | bytes 2097168 | tf_op jit(solution)/shard_map/all_gather | solution.py:31
  1119.7 2.8 fusion.12
  1122.5 40.4 %all-gather.1 = f32[64,2048]{1,0:T(8,128)S(1)} all-gather(f32[64,256]{1,0:T(8,128)S(1)} %fusion.12), channel_id=3, replica_groups=mesh['dp'=32,'fac'=8] {'fac'}, dimensions={1}, use_global_device_ids=true | all-gather | bytes 589824 | tf_op jit(solution)/shard_map/all_gather | solution.py:24
  1162.9 18.5 %all-gather.29.cloned.1.call-done = f32[1,2048,256]{2,1,0:T(8,128)} async-done(((f32[1,64,256]{2,1,0:T(8,128)}), f32[1,2048,256]{2,1,0:T(8,128)}) %all-gather.29.cloned.1.call-update) | async-done | bytes 2097168 | tf_op jit(solution)/shard_map/all_gather | solution.py:31
  1181.5 3.4 multiply_reduce_fusion
  1184.8 75.5 %psum.23 = f32[]{:T(128)} all-reduce(f32[]{:T(128)} %get-tuple-element.15), channel_id=1, replica_groups=mesh['dp'=32,'fac'=8] {'dp','fac'}, use_global_device_ids=true, to_apply=%region_11.12 | all-reduce | flops 1 | bytes 8 | tf_op jit(solution)/shard_map/psum | solution.py:103
  1261.0 0.6 broadcast_multiply_fusion
  (35 shorter events, 0.7 us)
Async XLA Ops:
  6.5 145.3 %copy-start = (bf16[2,2,256,256]{3,2,1,0:T(8,128)(2,1)S(1)}, bf16[2,2,256,256]{3,2,1,0:T(8,128)(2,1)}, u32[]{:S(2)}) copy-start(bf16[2,2,256,256]{3,2,1,0:T(8,128)(2,1)} %param.9) | copy-start | bytes 1572868
  6.5 65.8 %all-gather.17.cloned.1.call-start = ((), (), s32[]{:S(2)}) async-start(), calls=%async_computation.6 | async-start | bytes 1081344 | tf_op jit(solution)/shard_map/all_gather | solution.py:59
  7.3 141.9 %all-gather.15.cloned.1.call-start = ((), (), s32[]{:S(2)}) async-start(), calls=%async_computation.5 | async-start | bytes 2359296 | tf_op jit(solution)/shard_map/all_gather | solution.py:49
  8.0 216.4 %all-gather.13.cloned.1.call-start = ((), (), s32[]{:S(2)}) async-start(), calls=%async_computation.3 | async-start | bytes 2359296 | tf_op jit(solution)/shard_map/all_gather | solution.py:48
  8.7 290.9 %all-gather.19.cloned.1.call-start = ((), (), s32[]{:S(2)}) async-start(), calls=%async_computation.7 | async-start | bytes 2359296 | tf_op jit(solution)/shard_map/all_gather | solution.py:68
  151.8 74.9 %copy-start.4 = (f32[2048]{0:T(1024)S(1)}, f32[2048]{0:T(1024)}, u32[]{:S(2)}) copy-start(f32[2048]{0:T(1024)} %param.8) | copy-start | bytes 24580
  153.1 287.1 %reduce-scatter.4.cloned.1.call-start = ((), (), s32[]{:S(2)}) async-start(), calls=%async_computation.4 | async-start | bytes 2162688 | tf_op jit(solution)/shard_map/reduce_scatter | solution.py:84
  224.4 2.2 copy-start.1
  229.4 356.4 %reduce-scatter.6.cloned.1.call-start = ((), (), s32[]{:S(2)}) async-start(), calls=%async_computation.8 | async-start | bytes 2162688 | tf_op jit(solution)/shard_map/reduce_scatter | solution.py:85
  303.3 422.3 %all-gather.23.cloned.1.call-start = ((), (), s32[]{:S(2)}) async-start(), calls=%async_computation.10 | async-start | bytes 1179648 | tf_op jit(solution)/shard_map/all_gather | solution.py:24
  670.7 117.3 %all-gather.25.cloned.1.call-start = ((), (), s32[]{:S(2)}) async-start(), calls=%async_computation.11 | async-start | bytes 4325376 | tf_op jit(solution)/shard_map/all_gather | solution.py:31
  671.5 259.1 %reduce-scatter.8.cloned.1.call-start = ((), (), s32[]{:S(2)}) async-start(), calls=%async_computation.13 | async-start | bytes 2162688 | tf_op jit(solution)/shard_map/reduce_scatter | solution.py:86
  673.6 321.3 %all-gather.21.cloned.1.call-start = ((), (), s32[]{:S(2)}) async-start(), calls=%async_computation.9 | async-start | bytes 1179648 | tf_op jit(solution)/shard_map/all_gather | solution.py:24
  674.2 383.2 %copy-start.2 = (f32[2,64,256]{2,1,0:T(8,128)S(1)}, f32[2,64,256]{2,1,0:T(8,128)}, u32[]{:S(2)}) copy-start(f32[2,64,256]{2,1,0:T(8,128)} %get-tuple-element.12) | copy-start | bytes 393220
  674.2 383.2 %all-gather.27.cloned.1.call-start = ((), (), s32[]{:S(2)}) async-start(), calls=%async_computation.12 | async-start | bytes 4325376 | tf_op jit(solution)/shard_map/all_gather | solution.py:31
  793.8 325.9 %all-gather.31.cloned.1.call-start = ((), (), s32[]{:S(2)}) async-start(), calls=%async_computation.15 | async-start | bytes 2162688 | tf_op jit(solution)/shard_map/all_gather | solution.py:31
  930.5 250.9 %all-gather.29.cloned.1.call-start = ((), (), s32[]{:S(2)}) async-start(), calls=%async_computation.14 | async-start | bytes 2162688 | tf_op jit(solution)/shard_map/all_gather | solution.py:31
  1062.7 118.8 %copy-start.3 = (f32[64,256]{1,0:T(8,128)S(1)}, f32[64,256]{1,0:T(8,128)}, u32[]{:S(2)}) copy-start(f32[64,256]{1,0:T(8,128)} %reduce-scatter.8.cloned.1.call-done) | copy-start | bytes 196612
Sparse Core Ops, SparseCore 0:
  9.2 63.1 all-gather.16
  74.9 74.2 all-gather.14
  151.6 72.7 all-gather.12
  226.8 72.7 all-gather.18
  302.0 138.1 reduce-scatter.3
  442.7 143.0 reduce-scatter.5
  670.8 54.7 all-gather.22
  727.5 60.4 all-gather.24
  790.5 139.9 reduce-scatter.7
  933.2 61.7 all-gather.20
  997.0 60.4 all-gather.26
  1059.3 60.3 all-gather.30
  1121.7 59.6 all-gather.28
where the time goes:
time: 1270 us
  waiting for transfers between devices  977 us (77%)
  blocking collectives  237 us (19%)
  matrix products  27.9 us (2%)
  between operations  14.1 us (1%)
    all_gather x4, waiting for transfers between devices, panel_product(): lax.all_gather(right_block, 'dp', axis=1, tiled=True)  160 us
    reduce_scatter x1, waiting for transfers between devices, per_device(): lax.psum_scatter(g_part, 'dp', scatter_dimension=0, tiled=True)  146 us
    reduce_scatter x1, waiting for transfers between devices, per_device(): lax.psum_scatter(a_part, 'dp', scatter_dimension=0, tiled=True)  137 us
    reduce_scatter x1, waiting for transfers between devices, per_device(): lax.psum_scatter(grad_part, 'dp', scatter_dimension=0, tiled=True)  137 us
    all_gather x2, waiting for transfers between devices, panel_rows(): return lax.all_gather(block, 'fac', axis=2, tiled=True)  116 us
    psum x1, blocking collectives, per_device(): lax.psum((jnp.sum(a_block * a_block), jnp.sum(g_block * g_block)), ('dp',...  81.2 us
    all_gather x2, blocking collectives, panel_rows(): return lax.all_gather(block, 'fac', axis=2, tiled=True)  80.3 us
    all_gather x1, waiting for transfers between devices, per_device(): lax.all_gather(cotangent, 'fac', axis=1, tiled=True)  76.7 us
  transfers between devices with their start and end apart: 13, of which 13 were waited for; matrix products, arithmetic and copies ran while one was open for 2% of the time, Pallas kernels for 0%

commit v1 on v0

v1 whole, which is shorter than its diff:
```python
import jax
import jax.numpy as jnp
from jax import lax
from jax.experimental import pallas as pl
from jax.experimental.pallas import tpu as pltpu
from jax.sharding import PartitionSpec as P

ORBS = 256
NE = 48
TOK = 512
D = 2048
B = 256
R = 64
SCALE = 1.0 / 16384
damping = 0.1
epsilon = 1e-06
bf16 = jnp.bfloat16
f32 = jnp.float32
NSEM = 200


def dot(a, b):
    return lax.dot_general(a, b, (((1,), (0,)), ((), ())), preferred_element_type=f32)


def dot_t(a, b):
    return lax.dot_general(a, b, (((0,), (0,)), ((), ())), preferred_element_type=f32)


def kernel(occ, stream, gain, probs, w_out, cot, out,
           cot_all, st_all, n_all, v_all, w_all, acc, keep_s,
           part, rc_b, s1_b, rx_b, s2_b, rz_b, rzg_b, slab,
           grad_s, tsrc, tdst, tt, xg, xs, nrm_src, nrm, fin, ssem, rsem):
    d = lax.axis_index("dp")
    f = lax.axis_index("fac")
    z, x, c = d // 8, (d // 2) % 4, d % 2
    h, y = f // 4, f % 4

    def at(dh=0, dy=0, dz=0, dx=0, dc=0):
        nd = (((z + dz) % 4) * 4 + (x + dx) % 4) * 2 + (c + dc) % 2
        nf = ((h + dh) % 2) * 4 + (y + dy) % 4
        return {"dp": nd, "fac": nf}

    count = [0]
    started = []

    def copy(src, dst, dev):
        i = count[0]
        count[0] += 1
        return pltpu.make_async_remote_copy(
            src_ref=src, dst_ref=dst, send_sem=ssem.at[i], recv_sem=rsem.at[i],
            device_id=dev, device_id_type=pl.DeviceIdType.MESH)

    def start(cp):
        cp.start()
        started.append(cp)
        return cp

    fac_offs = [(a, b) for a in range(2) for b in range(4) if (a, b) != (0, 0)]
    dp_offs = [(a, b) for a in range(4) for b in range(4) if (a, b) != (0, 0)]

    bar = pltpu.get_barrier_semaphore()

    def greet(dev):
        pl.semaphore_signal(bar, inc=1, device_id=dev, device_id_type=pl.DeviceIdType.MESH)

    for a, b in fac_offs:
        greet(at(dh=a, dy=b))
    for a, b in dp_offs:
        greet(at(dz=a, dx=b))
    greet(at(dc=1))
    own = (d // 4) == f
    for m in range(4):
        @pl.when(jnp.logical_not(own & (d % 4 == m)))
        def _(m=m):
            greet({"dp": 4 * f + m, "fac": d // 4})
    pl.semaphore_wait(bar, 7 + 15 + 1 + 4 - own.astype(jnp.int32))

    class Gather:
        def __init__(self, src, buf):
            self.buf = buf
            self.first = [copy(src.at[pl.ds(k * 256, 256)], buf.at[f, pl.ds(k * 256, 256)], at(dh=1)) for k in range(2)]
            self.ring = [copy(src, buf.at[f], at(dy=j)) for j in (1, 3, 2)]
            other = (1 - h) * 4 + y
            self.fwd = [[copy(buf.at[other, pl.ds(k * 256, 256)], buf.at[other, pl.ds(k * 256, 256)], at(dy=j))
                         for j in (1, 3, 2)] for k in range(2)]

        def begin(self):
            for cp in self.first + self.ring:
                start(cp)

        def middle(self):
            for k in range(2):
                self.first[k].wait_recv()
                for cp in self.fwd[k]:
                    start(cp)

        def finish(self):
            for cp in self.ring + self.fwd[0] + self.fwd[1]:
                cp.wait_recv()

    g_cot = Gather(cot, cot_all)
    g_cot.begin()
    ii = lax.broadcasted_iota(jnp.int32, (R, R), 0)
    jj = lax.broadcasted_iota(jnp.int32, (R, R), 1)
    eye = (ii == jj).astype(bf16)
    w_all[z * 4 + x, c] = lax.dot_general(
        eye, w_out[...], (((1,), (1,)), ((), ())), preferred_element_type=f32).astype(bf16)
    w_me = w_all.at[z * 4 + x, c]
    w_cps = [start(copy(w_me, w_me, at(dz=a, dx=b))) for a, b in dp_offs]

    cot_all[f] = cot[...]
    row = lax.broadcasted_iota(jnp.int32, (ORBS, ORBS), 0)
    col = lax.broadcasted_iota(jnp.int32, (ORBS, ORBS), 1)
    pos = lax.broadcasted_iota(jnp.int32, (ORBS, 1), 0).astype(f32)
    for s in range(2):
        ones = occ[pl.ds(s, 1), :].astype(f32)
        before = jnp.sum(jnp.where(col < row, ones, 0.0), axis=1, keepdims=True)
        forced = (before == float(NE)) | (pos - before == float(ORBS - NE))
        keep_s[pl.ds(s * ORBS, ORBS), :] = jnp.where(forced, 0.0, 1.0)

    g_cot.middle()
    for cp in w_cps:
        cp.wait_recv()
    w_core = start(copy(w_all.at[:, c], w_all.at[:, c], at(dc=1)))
    g_st = Gather(stream, st_all)
    g_cot.finish()
    g_st.begin()
    st_all[f] = stream[...]
    w_core.wait_recv()

    acc[...] = jnp.zeros_like(acc)

    def og(b, _):
        w_blk = w_all[pl.ds(b * 2, 2)].reshape(B, B)
        acc[...] += dot(cot_all[b], w_blk)
        return 0

    lax.fori_loop(0, 8, og, 0)
    for s in range(2):
        rows = pl.ds(s * ORBS, ORBS)
        og_s = (acc[rows, :] * keep_s[rows, :]).astype(bf16)
        for hd in range(2):
            v = dot_t(probs[s, hd], og_s[:, hd * 128:(hd + 1) * 128])
            v_all[f, rows, pl.ds(hd * 128, 128)] = v.astype(bf16)
    g_v = Gather(v_all.at[f], v_all)
    g_v.begin()

    g_st.middle()
    g_v.middle()
    g_st.finish()

    def norm(t, _):
        rows = pl.ds(pl.multiple_of(t * 32, 32), 32)
        sq = jnp.zeros((32, B), f32)
        for b in range(8):
            v = st_all[b, rows, :].astype(f32)
            sq = sq + v * v
        inv = lax.rsqrt(jnp.sum(sq, axis=1, keepdims=True) * (1.0 / D) + epsilon)
        for b in range(8):
            v = st_all[b, rows, :].astype(f32)
            n_all[b, rows, :] = (v * inv * gain[:, b * B:(b + 1) * B]).astype(bf16)
        return 0

    lax.fori_loop(0, TOK // 32, norm, 0)

    def gram(k, left, right):
        def body(b, _):
            p = dot_t(left[b], right[f]) * SCALE
            part[k, pl.ds(b * 2, 2)] = p.astype(bf16).reshape(2, 2, R, B)
            return 0
        lax.fori_loop(0, 8, body, 0)

    core_cp = [copy(part.at[k, :, 1 - c], rc_b.at[k], at(dc=1)) for k in range(3)]
    x_cp = [[copy(s1_b.at[k, :, (x + j) % 4], rx_b.at[k, j - 1], at(dx=j)) for j in (1, 3, 2)] for k in range(3)]

    def core_done(k):
        core_cp[k].wait_recv()

        def body(q, _):
            s1_b[k, q] = (part[k, pl.ds(q * 4, 4), c].astype(f32)
                          + rc_b[k, pl.ds(q * 4, 4)].astype(f32)).astype(bf16)
            return 0
        lax.fori_loop(0, 4, body, 0)
        for cp in x_cp[k]:
            start(cp)

    z_cp = [[copy(s2_b.at[0, (z + j) % 4], rzg_b.at[j - 1], at(dz=j)) for j in (1, 3, 2)]]
    z_cp += [[copy(s2_b.at[k], rz_b.at[k - 1, j - 1], at(dz=j)) for j in (1, 3, 2)] for k in (1, 2)]

    def x_done(k):
        for cp in x_cp[k]:
            cp.wait_recv()
        t = s1_b[k, :, x].astype(f32)
        for j in range(3):
            t = t + rx_b[k, j].astype(f32)
        s2_b[k] = t.astype(bf16)
        for cp in z_cp[k]:
            start(cp)

    agx_cp = [[copy(slab.at[k, :, x, c], slab.at[k, :, x, c], at(dx=j)) for j in (1, 3, 2)] for k in range(2)]
    agc_cp = [copy(slab.at[k, :, :, c], slab.at[k, :, :, c], at(dc=1)) for k in range(2)]

    def z_done(k):
        for cp in z_cp[k]:
            cp.wait_recv()
        if k == 0:
            t = s2_b[0, z].astype(f32)
            for j in range(3):
                t = t + rzg_b[j].astype(f32)
            grad_s[...] = t
            return
        t = s2_b[k].astype(f32)
        for j in range(3):
            t = t + rz_b[k - 1, j].astype(f32)
        slab[k - 1, :, x, c] = t.astype(bf16)
        for cp in agx_cp[k - 1]:
            start(cp)

    def agx_done(k):
        for cp in agx_cp[k - 1]:
            cp.wait_recv()
        start(agc_cp[k - 1])

    nrm_cp = [[copy(nrm_src.at[k], nrm.at[k, f], at(dh=a, dy=b)) for a, b in fac_offs] for k in range(2)]

    def agc_done(k):
        agc_cp[k - 1].wait_recv()

        def body(b, t):
            blk = slab[k - 1, b // 2, pl.ds((b % 2) * 2, 2)].reshape(B, B).astype(f32)
            add = jnp.where((row == col) & (b == f), damping, 0.0)
            blk = blk + add
            return t + jnp.sum(blk * blk, axis=0, keepdims=True)
        t = lax.fori_loop(0, 8, body, jnp.zeros((1, B), f32))
        total = jnp.sum(t, axis=1, keepdims=True)
        nrm_src[k - 1] = jnp.broadcast_to(total, (8, 128))
        nrm[k - 1, f] = jnp.broadcast_to(total, (8, 128))
        for cp in nrm_cp[k - 1]:
            start(cp)

    def alpha_of(k):
        for cp in nrm_cp[k - 1]:
            cp.wait_recv()
        t = nrm[k - 1, 0]
        for b in range(1, 8):
            t = t + nrm[k - 1, b]
        return (1.0 / jnp.sqrt(t))[0:1, 0:1]

    x_own = [None] * 6
    step_cp = [[copy(xs.at[i], xg.at[i, f], at(dh=a, dy=b)) for a, b in fac_offs] for i in range(6)]

    def step_send(i, value):
        v = value.astype(bf16)
        xs[i] = v
        xg[i, f] = v
        x_own[i] = value
        for cp in step_cp[i]:
            start(cp)

    def step_mul(i, k):
        for cp in step_cp[i]:
            cp.wait_recv()
        t = x_own[i] * damping
        for b in range(8):
            t = t + dot(xg[i, b], slab[k - 1, b // 2, (b % 2) * 2:(b % 2) * 2 + 2].reshape(B, B))
        return t

    t_base = []
    for _ in range(2):
        t_base.append(count[0])
        count[0] += 4
    peers = {"fac": d // 4}

    def t_copy(i, m, slot):
        return pltpu.make_async_remote_copy(
            src_ref=tsrc.at[i, m // 2], dst_ref=tdst.at[i, slot], send_sem=ssem.at[t_base[i] + m],
            recv_sem=rsem.at[t_base[i] + slot], device_id={"dp": 4 * f + m, "fac": d // 4},
            device_id_type=pl.DeviceIdType.MESH)

    def t_send(i, value):
        tsrc[i, 0] = value[:, :128]
        tsrc[i, 1] = value[:, 128:]
        slot = d % 4
        for m in range(4):
            here = own & (d % 4 == m)

            @pl.when(here)
            def _(m=m):
                pltpu.make_async_copy(tsrc.at[i, m // 2], tdst.at[i, slot], rsem.at[t_base[i] + slot]).start()

            @pl.when(jnp.logical_not(here))
            def _(m=m):
                t_copy(i, m, slot).start()

    def t_recv(i):
        for k in range(4):
            t_copy(i, k, k).wait_recv()
        s = jnp.concatenate([tdst[i, k] for k in range(4)], axis=0)
        tt[...] = s.T
        return tt[pl.ds(pl.multiple_of((d % 2) * R, R), R), :]

    gram(0, n_all, v_all)
    start(core_cp[0])
    gram(1, n_all, n_all)
    start(core_cp[1])
    core_done(0)
    core_done(1)
    g_v.finish()
    gram(2, v_all, v_all)
    start(core_cp[2])
    x_done(0)
    x_done(1)
    core_done(2)
    z_done(0)
    t_send(0, grad_s[...])
    z_done(1)
    x_done(2)
    agx_done(1)
    x0 = t_recv(0)
    agc_done(1)
    step_send(0, x0)
    z_done(2)
    a_alpha = alpha_of(1)
    c1 = 4.0 * x0 - a_alpha * step_mul(0, 1)
    step_send(1, c1)
    agx_done(2)
    c2 = 6.0 * x0 - a_alpha * step_mul(1, 1)
    step_send(2, c2)
    agc_done(2)
    c3 = 4.0 * x0 - a_alpha * step_mul(2, 1)
    t_send(1, c3)
    g_alpha = alpha_of(2)
    l0 = t_recv(1)
    step_send(3, l0)
    c1 = 4.0 * l0 - g_alpha * step_mul(3, 2)
    step_send(4, c1)
    c2 = 6.0 * l0 - g_alpha * step_mul(4, 2)
    step_send(5, c2)
    c3 = 4.0 * l0 - g_alpha * step_mul(5, 2)
    pre = c3 * (a_alpha * g_alpha)

    part_sum = jnp.sum(jnp.sum(grad_s[...] * pre, axis=0, keepdims=True), axis=1, keepdims=True)
    fin[0] = jnp.broadcast_to(part_sum, (8, 128))
    cp = start(copy(fin.at[0], fin.at[1], at(dc=1)))
    cp.wait_recv()
    fin[2] = fin[0] + fin[1]
    cps = [start(copy(fin.at[2], fin.at[3 + i], at(dz=a, dx=b))) for i, (a, b) in enumerate(dp_offs)]
    for cp in cps:
        cp.wait_recv()
    t = fin[2]
    for i in range(15):
        t = t + fin[3 + i]
    fin[18] = t
    cps = [start(copy(fin.at[18], fin.at[19 + i], at(dh=a, dy=b))) for i, (a, b) in enumerate(fac_offs)]
    for cp in cps:
        cp.wait_recv()
    for i in range(7):
        t = t + fin[19 + i]
    inner = t[0:1, 0:1]
    out[...] = pre * (float(D) / jnp.sqrt(inner + epsilon))

    for cp in started:
        cp.wait_send()
    for i in range(2):
        for m in range(4):
            @pl.when(jnp.logical_not(own & (d % 4 == m)))
            def _(i=i, m=m):
                t_copy(i, m, 0).wait_send()
    assert count[0] <= NSEM


def per_device(occupations, stream, norm_gain, probs, w_out, cotangent):
    vm = pl.BlockSpec(memory_space=pltpu.VMEM)
    V = pltpu.VMEM
    return pl.pallas_call(
        kernel,
        out_shape=jax.ShapeDtypeStruct((R, B), f32),
        in_specs=[vm] * 6,
        out_specs=vm,
        scratch_shapes=[
            V((8, TOK, B), bf16),
            V((8, TOK, B), bf16),
            V((8, TOK, B), bf16),
            V((8, TOK, B), bf16),
            V((16, 2, R, B), bf16),
            V((TOK, B), f32),
            V((TOK, 1), f32),
            V((3, 16, 2, R, B), bf16),
            V((3, 16, R, B), bf16),
            V((3, 4, 4, R, B), bf16),
            V((3, 3, 4, R, B), bf16),
            V((3, 4, R, B), bf16),
            V((2, 3, 4, R, B), bf16),
            V((3, R, B), bf16),
            V((2, 4, 4, 2, R, B), bf16),
            V((R, B), f32),
            V((2, 2, R, 128), f32),
            V((2, 4, R, 128), f32),
            V((128, B), f32),
            V((6, 8, R, B), bf16),
            V((6, R, B), bf16),
            V((2, 8, 128), f32),
            V((2, 8, 8, 128), f32),
            V((26, 8, 128), f32),
            pltpu.SemaphoreType.DMA((NSEM,)),
            pltpu.SemaphoreType.DMA((NSEM,)),
        ],
        compiler_params=pltpu.CompilerParams(
            collective_id=0, has_side_effects=True, vmem_limit_bytes=56 << 20),
    )(occupations, stream, norm_gain.reshape(1, D), probs, w_out, cotangent)


def solution(mesh):
    placed = (
        P("dp", None),
        P("dp", "fac"),
        P(),
        P("dp", "fac", None, None),
        P("fac", "dp"),
        P("dp", "fac"),
    )
    return jax.shard_map(
        per_device, mesh=mesh, in_specs=placed, out_specs=P("dp", "fac"), check_vma=False
    )
```

time: 1270 us -> 208 us (0.16)
  waiting for transfers between devices: 977 us -> 0 us
  blocking collectives: 237 us -> 0 us
  Pallas kernels: 0 us -> 204 us
  matrix products: 27.9 us -> 0 us
  between operations: 14.1 us -> 0.01 us
    all_gather x10 -> x0, waiting for transfers between devices: 555 us -> none  [the longest x4 160 us: panel_product(): lax.all_gather(right_block, 'dp', axis=1, tiled=True)]
    reduce_scatter x3 -> x0, waiting for transfers between devices: 419 us -> none  [the longest x1 146 us: per_device(): lax.psum_scatter(g_part, 'dp', scatter_dimension=0, tiled=True)]
    pallas_call x0 -> x1, Pallas kernels: none -> 204 us  [per_device(): pl.pallas_call(kernel, out_shape=jax.ShapeDtypeStruct((R, B), f32), in_sp...]
    psum x2 -> x0, blocking collectives: 157 us -> none  [the longest x1 81.2 us: per_device(): lax.psum((jnp.sum(a_block * a_block), jnp.sum(g_block * g_block)), ('dp',...]
    all_gather x2 -> x0, blocking collectives: 80.3 us -> none  [panel_rows(): return lax.all_gather(block, 'fac', axis=2, tiled=True)]
    dot_general x9 -> x0, matrix products: 27.9 us -> none  [the longest x4 17.1 us: panel_product(): jnp.einsum('brk,bkc->brc', left_rows, lax.all_gather(right_block, 'dp', a...]
  transfers between devices with their start and end apart: 13 -> 0, of which waited for: 13 -> 0; matrix products, arithmetic and copies ran while one was open for 2% -> 0% of each run, Pallas kernels for 0% -> 0%
where the time goes in v1:
time: 208 us; the launch traced here: 207 us
  Pallas kernels  204 us (98%)
  local copies, waits for them, and re-layouts  2.96 us (1%)
    pallas_call x1, Pallas kernels, per_device(): pl.pallas_call(kernel, out_shape=jax.ShapeDtypeStruct((R, B), f32), in_sp...  204 us

profile of v1, /device:TPU:1, one launch (start us, length us, event | category | flops | bytes accessed | tf_op | source)
XLA Modules:
  0.0 207.4 jit_solution(9254677508076388383)
XLA Ops:
  0.0 1.5 copy.7.w_out
  1.5 204.4 %shard_map.64 = f32[64,256]{1,0:T(8,128)} custom-call(s32[2,256]{1,0:T(2,128)} %occ.1, bf16[512,256]{1,0:T(8,128)(2,1)} %stream.1, f32[1,2048]{1,0:T(1,128)} %bitcast.1, bf16[2,2,256,256]{3,2,1,0:T(8,128)(2,1)} %probs.1, bf16[256,64]{1,0:T(8,128)(2,1)} %copy.7.w_out, bf16[512,256]{1,0:T(8,128)(2,1)} %cot.1), custom_call_target="tpu_custom_call" | custom-call | tf_op jit(solution)/shard_map/pallas_call | solution.py:376
  205.9 1.5 copy.9

commit v2 on v1

v2 whole, which is shorter than its diff:
```python
import jax
import jax.numpy as jnp
from jax import lax
from jax.experimental import pallas as pl
from jax.experimental.pallas import tpu as pltpu
from jax.sharding import PartitionSpec as P

ORBS = 256
NE = 48
TOK = 512
D = 2048
B = 256
R = 64
SCALE = 1.0 / 16384
damping = 0.1
epsilon = 1e-06
bf16 = jnp.bfloat16
f32 = jnp.float32
NSEM = 240


def dot(a, b):
    return lax.dot_general(a, b, (((1,), (0,)), ((), ())), preferred_element_type=f32)


def dot_t(a, b):
    return lax.dot_general(a, b, (((0,), (0,)), ((), ())), preferred_element_type=f32)


def kernel(occ, stream_h, gain, probs_h, w_h, cot_h, out,
           cot_all, st_all, n_all, v_all, w_all, probs, acc, keep_s,
           part, rc_b, s1_b, rx_b, s2_b, rz_b, slab,
           grad2, gx, tsrc, tdst, tt, xg, nsrc, nbuf, fin, lsem, ssem, rsem):
    d = lax.axis_index("dp")
    f = lax.axis_index("fac")
    z, x, c = d // 8, (d // 2) % 4, d % 2
    h, y = f // 4, f % 4
    fd = d // 4
    mesh_id = pl.DeviceIdType.MESH

    def at(dh=0, dy=0, dz=0, dx=0, dc=0):
        nd = (((z + dz) % 4) * 4 + (x + dx) % 4) * 2 + (c + dc) % 2
        nf = ((h + dh) % 2) * 4 + (y + dy) % 4
        return {"dp": nd, "fac": nf}

    count = [0]
    started = []

    def copy(src, dst, dev):
        i = count[0]
        count[0] += 1
        return pltpu.make_async_remote_copy(
            src_ref=src, dst_ref=dst, send_sem=ssem.at[i], recv_sem=rsem.at[i],
            device_id=dev, device_id_type=pl.DeviceIdType.MESH)

    def start(cp):
        cp.start()
        started.append(cp)
        return cp

    fac_offs = [(1, 2), (1, 1), (1, 3), (1, 0), (0, 2), (0, 1), (0, 3)]
    dp_offs = [(a, b) for a in range(4) for b in range(4) if (a, b) != (0, 0)]
    z8_offs = [(1, 0), (1, 1), (1, 2), (1, 3), (0, 2), (0, 1), (0, 3)]

    bar = pltpu.get_barrier_semaphore()

    def greet(dev):
        pl.semaphore_signal(bar, inc=1, device_id=dev, device_id_type=mesh_id)

    for a, b in fac_offs:
        greet(at(dh=a, dy=b))
    for a, b in dp_offs:
        greet(at(dz=a, dx=b))
    greet(at(dc=1))
    for j in (1, 2, 3):
        greet(at(dh=1, dz=j))
    own0 = fd == f
    own1 = fd % 4 == y
    for e in range(2):
        for m in range(4):
            me = d == 4 * (e * 4 + y) + m

            @pl.when(jnp.logical_not(own0 & me))
            def _(e=e, m=m):
                greet({"dp": 4 * (e * 4 + y) + m, "fac": fd})

            @pl.when(jnp.logical_not(own1 & me))
            def _(e=e, m=m):
                greet({"dp": 4 * (e * 4 + y) + m, "fac": h * 4 + fd % 4})

    local = [pltpu.make_async_copy(a, b, lsem.at[i]) for i, (a, b) in enumerate([
        (stream_h, st_all.at[f]), (cot_h, cot_all.at[f]), (w_h, w_all.at[z * 4 + x, c]), (probs_h, probs)])]
    for cp in local:
        cp.start()
    pl.semaphore_wait(bar, 7 + 15 + 1 + 3 + 16 - own0.astype(jnp.int32) - own1.astype(jnp.int32))

    class Gather:
        def __init__(self, buf):
            other = (1 - h) * 4 + y
            rows = [pl.ds(k * 256, 256) for k in range(2)]
            self.first = [copy(buf.at[f, r], buf.at[f, r], at(dh=1)) for r in rows]
            self.ring = [copy(buf.at[f], buf.at[f], at(dy=j)) for j in (1, 3, 2)]
            self.fwd = [[copy(buf.at[other, r], buf.at[other, r], at(dy=j)) for j in (1, 3, 2)] for r in rows]

        def begin_z(self):
            for cp in self.first:
                start(cp)

        def begin_y(self):
            for cp in self.ring:
                start(cp)

        def middle(self):
            for k in range(2):
                self.first[k].wait_recv()
                for cp in self.fwd[k]:
                    start(cp)

        def finish_a(self):
            for cp in self.ring + self.fwd[0]:
                cp.wait_recv()

        def finish_b(self):
            for cp in self.fwd[1]:
                cp.wait_recv()

    g_st, g_cot, g_v = Gather(st_all), Gather(cot_all), Gather(v_all)
    local[0].wait()
    g_st.begin_z()
    g_st.begin_y()
    row = lax.broadcasted_iota(jnp.int32, (ORBS, ORBS), 0)
    col = lax.broadcasted_iota(jnp.int32, (ORBS, ORBS), 1)
    pos = lax.broadcasted_iota(jnp.int32, (ORBS, 1), 0).astype(f32)
    for s in range(2):
        ones = occ[pl.ds(s, 1), :].astype(f32)
        before = jnp.sum(jnp.where(col < row, ones, 0.0), axis=1, keepdims=True)
        forced = (before == float(NE)) | (pos - before == float(ORBS - NE))
        keep_s[pl.ds(s * ORBS, ORBS), :] = jnp.where(forced, 0.0, 1.0)
    for cp in local[1:]:
        cp.wait()
    g_st.middle()
    g_cot.begin_z()
    w_me = w_all.at[z * 4 + x, c]
    w_cps = [start(copy(w_me, w_me, at(dz=a, dx=b))) for a, b in dp_offs]
    w_core = copy(w_all.at[:, c], w_all.at[:, c], at(dc=1))
    g_st.finish_a()
    g_cot.begin_y()
    g_st.finish_b()

    def norm(t, _):
        rows = pl.ds(pl.multiple_of(t * 32, 32), 32)
        sq = jnp.zeros((32, B), f32)
        for b in range(8):
            v = st_all[b, rows, :].astype(f32)
            sq = sq + v * v
        inv = lax.rsqrt(jnp.sum(sq, axis=1, keepdims=True) * (1.0 / D) + epsilon)
        for b in range(8):
            v = st_all[b, rows, :].astype(f32)
            n_all[b, rows, :] = (v * inv * gain[:, b * B:(b + 1) * B]).astype(bf16)
        return 0

    def gram(k, left, right):
        def body(b, _):
            p = dot_t(left[b], right[f]) * SCALE
            part[k, pl.ds(b * 2, 2)] = p.astype(bf16).reshape(2, 2, R, B)
            return 0
        lax.fori_loop(0, 8, body, 0)

    core_cp = [copy(part.at[k, :, 1 - c], rc_b.at[k], at(dc=1)) for k in range(3)]
    x_cp = [[copy(s1_b.at[k, :, (x + j) % 4], rx_b.at[k, j - 1], at(dx=j)) for j in (1, 3, 2)] for k in range(3)]

    def core_done(k):
        core_cp[k].wait_recv()

        def body(q, _):
            s1_b[k, q] = (part[k, pl.ds(q * 4, 4), c].astype(f32)
                          + rc_b[k, pl.ds(q * 4, 4)].astype(f32)).astype(bf16)
            return 0
        lax.fori_loop(0, 4, body, 0)
        for cp in x_cp[k]:
            start(cp)

    z_cp = [[copy(s2_b.at[k, (z + j) % 4], rz_b.at[k, j - 1], at(dz=j)) for j in (2, 1, 3)] for k in range(3)]

    def x_done(k):
        for cp in x_cp[k]:
            cp.wait_recv()
        t = s1_b[k, :, x].astype(f32)
        for j in range(3):
            t = t + rx_b[k, j].astype(f32)
        s2_b[k] = t.astype(bf16)
        for cp in z_cp[k]:
            start(cp)

    agz_cp = [[copy(slab.at[k, h, z, x, c], slab.at[k, h, z, x, c], at(dh=a, dz=b)) for a, b in z8_offs] for k in range(2)]
    agx_cp = [[copy(slab.at[k, :, :, x, c], slab.at[k, :, :, x, c], at(dx=j)) for j in (1, 3, 2)] for k in range(2)]
    agc_cp = [copy(slab.at[k, :, :, :, c], slab.at[k, :, :, :, c], at(dc=1)) for k in range(2)]
    nz_cp = [[copy(nsrc.at[k, 0], nbuf.at[k, i], at(dh=a, dz=b)) for i, (a, b) in enumerate(z8_offs)] for k in range(2)]
    nx_cp = [[copy(nsrc.at[k, 1], nbuf.at[k, 7 + i], at(dx=j)) for i, j in enumerate((1, 3, 2))] for k in range(2)]
    nc_cp = [[copy(nsrc.at[k, 2], nbuf.at[k, 10], at(dc=1))] for k in range(2)]
    ny_cp = [[copy(nsrc.at[k, 3], nbuf.at[k, 11 + i], at(dy=j)) for i, j in enumerate((1, 3, 2))] for k in range(2)]

    def total(v):
        return jnp.broadcast_to(
            jnp.sum(jnp.sum(v, axis=0, keepdims=True), axis=1, keepdims=True), (8, 128))

    def gathered(k, cps, nst, first, n):
        for cp in cps:
            cp.wait_recv()
        t = nsrc[k, nst]
        for i in range(n):
            t = t + nbuf[k, first + i]
        nsrc[k, nst + 1] = t

    grad_part = copy(grad2.at[h], grad2.at[h], at(dh=1))
    gx_cp = [copy(gx.at[f], gx.at[f], at(dh=a, dy=b)) for a, b in fac_offs]

    def z_done(k):
        for cp in z_cp[k]:
            cp.wait_recv()
        t = s2_b[k, z].astype(f32)
        for j in range(3):
            t = t + rz_b[k, j].astype(f32)
        if k == 0:
            grad2[h] = t
            return t
        slab[k - 1, h, z, x, c] = t.astype(bf16)
        ri = d * R + lax.broadcasted_iota(jnp.int32, (R, B), 0)
        ci = f * B + lax.broadcasted_iota(jnp.int32, (R, B), 1)
        t = t + jnp.where(ri == ci, damping, 0.0)
        nsrc[k - 1, 0] = total(t * t)
        for cp in agz_cp[k - 1] + nz_cp[k - 1]:
            start(cp)
        return None

    def agz_done(k):
        gathered(k - 1, agz_cp[k - 1] + nz_cp[k - 1], 0, 0, 7)
        for cp in agx_cp[k - 1] + nx_cp[k - 1]:
            start(cp)

    def agx_done(k):
        gathered(k - 1, agx_cp[k - 1] + nx_cp[k - 1], 1, 7, 3)
        for cp in [agc_cp[k - 1]] + nc_cp[k - 1]:
            start(cp)

    def agc_done(k):
        gathered(k - 1, [agc_cp[k - 1]] + nc_cp[k - 1], 2, 10, 1)
        for cp in ny_cp[k - 1]:
            start(cp)

    def alpha_of(k):
        for cp in ny_cp[k - 1]:
            cp.wait_recv()
        t = nsrc[k - 1, 3]
        for i in range(3):
            t = t + nbuf[k - 1, 11 + i]
        return (1.0 / jnp.sqrt(t))[0:1, 0:1]

    def slab_rows(k, e, b):
        return slab[k - 1, e, b // 2, (b % 2) * 2:(b % 2) * 2 + 2].reshape(B, B)

    def both(k, block):
        cols = []
        for e in range(2):
            t = dot(block(0), slab_rows(k, e, 0))
            for b in range(1, 8):
                t = t + dot(block(b), slab_rows(k, e, b))
            cols.append(t)
        return jnp.concatenate(cols, axis=1)

    x_own = [None] * 6
    step_cp = [[copy(xg.at[i, y], xg.at[i, y], at(dy=j)) for j in (2, 1, 3)] for i in range(6)]

    def step_send(i, value):
        v = value.astype(bf16)
        xg[i, y, 0] = v[:, :B]
        xg[i, y, 1] = v[:, B:]
        x_own[i] = value
        for cp in step_cp[i]:
            start(cp)

    def step_mul(i, k):
        for cp in step_cp[i]:
            cp.wait_recv()
        return x_own[i] * damping + both(k, lambda b: xg[i, b % 4, b // 4])

    t_base = []
    for _ in range(2):
        t_base.append(count[0])
        count[0] += 8
    t_slot = (fd // 4) * 4 + d % 4

    def t_copy(i, e, m, slot):
        if i == 0:
            dev = {"dp": 4 * f + m, "fac": e * 4 + fd % 4}
        else:
            dev = {"dp": 4 * (e * 4 + y) + m, "fac": h * 4 + fd % 4}
        return pltpu.make_async_remote_copy(
            src_ref=tsrc.at[i, 0 if i == 0 else e, m // 2], dst_ref=tdst.at[i, slot],
            send_sem=ssem.at[t_base[i] + e * 4 + m], recv_sem=rsem.at[t_base[i] + slot],
            device_id=dev, device_id_type=pl.DeviceIdType.MESH)

    def t_here(i, e, m):
        if i == 0:
            return own0 & (d == 4 * f + m) & (h == e)
        return own1 & (d == 4 * (e * 4 + y) + m)

    def t_send(i, value):
        for e in range(value.shape[1] // B):
            for q in range(2):
                tsrc[i, e, q] = value[:, e * B + q * 128:e * B + (q + 1) * 128]
        for e in range(2):
            for m in range(4):
                here = t_here(i, e, m)

                @pl.when(here)
                def _(e=e, m=m):
                    pltpu.make_async_copy(
                        tsrc.at[i, 0 if i == 0 else e, m // 2], tdst.at[i, t_slot],
                        rsem.at[t_base[i] + t_slot]).start()

                @pl.when(jnp.logical_not(here))
                def _(e=e, m=m):
                    t_copy(i, e, m, t_slot).start()

    def t_recv(i):
        for k in range(8):
            t_copy(i, k // 4, k % 4, k).wait_recv()
        for e in range(2):
            s = jnp.concatenate([tdst[i, e * 4 + k] for k in range(4)], axis=0)
            tt[:, e * B:(e + 1) * B] = s.T
        return tt[pl.ds(pl.multiple_of((d % 2) * R, R), R), :]

    lax.fori_loop(0, TOK // 32, norm, 0)
    gram(1, n_all, n_all)
    start(core_cp[1])
    g_cot.middle()
    for cp in w_cps:
        cp.wait_recv()
    start(w_core)
    core_done(1)
    g_cot.finish_a()
    g_cot.finish_b()
    w_core.wait_recv()

    acc[...] = jnp.zeros_like(acc)

    def og(b, _):
        w_blk = w_all[pl.ds(b * 2, 2)].reshape(B, B)
        acc[...] += dot(cot_all[b], w_blk)
        return 0

    lax.fori_loop(0, 8, og, 0)
    for s in range(2):
        rows = pl.ds(s * ORBS, ORBS)
        og_s = (acc[rows, :] * keep_s[rows, :]).astype(bf16)
        for hd in range(2):
            v = dot_t(probs[s, hd], og_s[:, hd * 128:(hd + 1) * 128])
            v_all[f, rows, pl.ds(hd * 128, 128)] = v.astype(bf16)
    g_v.begin_z()
    g_v.begin_y()
    gram(0, n_all, v_all)
    start(core_cp[0])
    x_done(1)
    core_done(0)
    z_done(1)
    g_v.middle()
    x_done(0)
    agz_done(1)
    g_v.finish_a()
    g_v.finish_b()
    gram(2, v_all, v_all)
    start(core_cp[2])
    grad = z_done(0)
    t_send(0, grad)
    gx[f] = grad.astype(bf16)
    for cp in gx_cp + [grad_part]:
        start(cp)
    core_done(2)
    agx_done(1)
    x0 = t_recv(0)
    step_send(0, x0)
    agc_done(1)
    x_done(2)
    a_alpha = alpha_of(1)
    c1 = 4.0 * x0 - a_alpha * step_mul(0, 1)
    step_send(1, c1)
    z_done(2)
    c2 = 6.0 * x0 - a_alpha * step_mul(1, 1)
    step_send(2, c2)
    agz_done(2)
    c3 = 4.0 * x0 - a_alpha * step_mul(2, 1)
    t_send(1, c3)
    agx_done(2)
    l0 = t_recv(1)
    step_send(3, l0)
    for cp in gx_cp + [grad_part]:
        cp.wait_recv()
    agc_done(2)
    q0 = both(2, lambda b: gx[b])
    g_alpha = alpha_of(2)
    grads = jnp.concatenate([grad2[0], grad2[1]], axis=1)
    q0 = q0 + damping * grads
    c1 = 4.0 * l0 - g_alpha * step_mul(3, 2)
    step_send(4, c1)
    c2 = 6.0 * l0 - g_alpha * step_mul(4, 2)
    step_send(5, c2)

    fin[0] = total(4.0 * grads * l0 - g_alpha * (q0 * c2))
    fc = start(copy(fin.at[0], fin.at[1], at(dc=1)))
    fx = [copy(fin.at[2], fin.at[3 + i], at(dz=a, dx=b)) for i, (a, b) in enumerate(dp_offs)]
    fy = [copy(fin.at[18], fin.at[19 + i], at(dy=j)) for i, j in enumerate((2, 1, 3))]
    fc.wait_recv()
    fin[2] = fin[0] + fin[1]
    for cp in fx:
        start(cp)
    c3 = 4.0 * l0 - g_alpha * step_mul(5, 2)
    ab = a_alpha * g_alpha
    for cp in fx:
        cp.wait_recv()
    t = fin[2]
    for i in range(15):
        t = t + fin[3 + i]
    fin[18] = t
    for cp in fy:
        start(cp)
    tt[0:R, :] = c3 * ab
    for cp in fy:
        cp.wait_recv()
    for i in range(3):
        t = t + fin[19 + i]
    inner = t[0:1, 0:1] * ab
    out[...] = tt[0:R, pl.ds(pl.multiple_of(h * B, B), B)] * (float(D) / jnp.sqrt(inner + epsilon))

    for cp in started:
        cp.wait_send()
    for i in range(2):
        for e in range(2):
            for m in range(4):
                @pl.when(jnp.logical_not(t_here(i, e, m)))
                def _(i=i, e=e, m=m):
                    t_copy(i, e, m, 0).wait_send()
    assert count[0] <= NSEM


def per_device(occupations, stream, norm_gain, probs, w_out, cotangent):
    vm = pl.BlockSpec(memory_space=pltpu.VMEM)
    hb = pl.BlockSpec(memory_space=pl.ANY)
    V = pltpu.VMEM
    return pl.pallas_call(
        kernel,
        out_shape=jax.ShapeDtypeStruct((R, B), f32),
        in_specs=[vm, hb, vm, hb, hb, hb],
        out_specs=vm,
        scratch_shapes=[
            V((8, TOK, B), bf16),
            V((8, TOK, B), bf16),
            V((8, TOK, B), bf16),
            V((8, TOK, B), bf16),
            V((16, 2, R, B), bf16),
            V((2, 2, ORBS, ORBS), bf16),
            V((TOK, B), f32),
            V((TOK, 1), f32),
            V((3, 16, 2, R, B), bf16),
            V((3, 16, R, B), bf16),
            V((3, 4, 4, R, B), bf16),
            V((3, 3, 4, R, B), bf16),
            V((3, 4, R, B), bf16),
            V((3, 3, R, B), bf16),
            V((2, 2, 4, 4, 2, R, B), bf16),
            V((2, R, B), f32),
            V((8, R, B), bf16),
            V((2, 2, 2, R, 128), f32),
            V((2, 8, R, 128), f32),
            V((128, 2 * B), f32),
            V((6, 4, 2, R, B), bf16),
            V((2, 4, 8, 128), f32),
            V((2, 14, 8, 128), f32),
            V((22, 8, 128), f32),
            pltpu.SemaphoreType.DMA((4,)),
            pltpu.SemaphoreType.DMA((NSEM,)),
            pltpu.SemaphoreType.DMA((NSEM,)),
        ],
        compiler_params=pltpu.CompilerParams(
            collective_id=0, has_side_effects=True, vmem_limit_bytes=56 << 20),
    )(occupations, stream, norm_gain.reshape(1, D), probs, w_out.T, cotangent)


def solution(mesh):
    placed = (
        P("dp", None),
        P("dp", "fac"),
        P(),
        P("dp", "fac", None, None),
        P("fac", "dp"),
        P("dp", "fac"),
    )
    return jax.shard_map(
        per_device, mesh=mesh, in_specs=placed, out_specs=P("dp", "fac"), check_vma=False
    )
```

time: 208 us -> 183 us (0.88)
  Pallas kernels: 204 us -> 182 us
    pallas_call x1, Pallas kernels: 204 us -> 182 us  [per_device(): pl.pallas_call(kernel, out_shape=jax.ShapeDtypeStruct((R, B), f32), in_sp...]
where the time goes in v2:
time: 183 us
  Pallas kernels  182 us (99%)
    pallas_call x1, Pallas kernels, per_device(): pl.pallas_call(kernel, out_shape=jax.ShapeDtypeStruct((R, B), f32), in_sp...  182 us

profile of v2, /device:TPU:1, one launch (start us, length us, event | category | flops | bytes accessed | tf_op | source)
XLA Modules:
  0.0 183.0 jit_solution(4426127059741329399)
XLA Ops:
  0.0 181.5 %shard_map.64 = f32[64,256]{1,0:T(8,128)} custom-call(s32[2,256]{1,0:T(2,128)} %occ.1, bf16[512,256]{1,0:T(8,128)(2,1)} %stream_h.1, f32[1,2048]{1,0:T(1,128)} %bitcast.3, bf16[2,2,256,256]{3,2,1,0:T(8,128)(2,1)} %probs_h.1, bf16[64,256]{1,0:T(8,128)(2,1)} %bitcast.2, bf16[512,256]{1,0:T(8,128)(2,1)} %cot_h.1), custom_call_target="tpu_custom_call" | custom-call | tf_op jit(solution)/shard_map/pallas_call | solution.py:450
  181.6 1.5 copy.8

commit v3 on v2

--- a/solution.py
+++ b/solution.py
@@ -30,7 +30,7 @@
 def kernel(occ, stream_h, gain, probs_h, w_h, cot_h, out,
            cot_all, st_all, n_all, v_all, w_all, probs, acc, keep_s,
            part, rc_b, s1_b, rx_b, s2_b, rz_b, slab,
-           grad2, gx, tsrc, tdst, tt, xg, nsrc, nbuf, fin, lsem, ssem, rsem):
+           grad2, gx, tp, tpo, tsrc, tdst, tt, xg, nsrc, nbuf, fin, lsem, ssem, rsem):
     d = lax.axis_index("dp")
     f = lax.axis_index("fac")
     z, x, c = d // 8, (d // 2) % 4, d % 2
@@ -76,52 +76,70 @@
         greet(at(dh=1, dz=j))
     own0 = fd == f
     own1 = fd % 4 == y
+    pair = x % 2
     for e in range(2):
-        for m in range(4):
-            me = d == 4 * (e * 4 + y) + m
-
-            @pl.when(jnp.logical_not(own0 & me))
-            def _(e=e, m=m):
-                greet({"dp": 4 * (e * 4 + y) + m, "fac": fd})
-
-            @pl.when(jnp.logical_not(own1 & me))
-            def _(e=e, m=m):
-                greet({"dp": 4 * (e * 4 + y) + m, "fac": h * 4 + fd % 4})
+        for kk in range(2):
+            src_d = 4 * (e * 4 + y) + 2 * kk + pair
+
+            @pl.when(jnp.logical_not(own0 & (d == src_d)))
+            def _(src_d=src_d):
+                greet({"dp": src_d, "fac": fd})
+
+            @pl.when(jnp.logical_not(own1 & (d == src_d)))
+            def _(src_d=src_d):
+                greet({"dp": src_d, "fac": h * 4 + fd % 4})
 
     local = [pltpu.make_async_copy(a, b, lsem.at[i]) for i, (a, b) in enumerate([
         (stream_h, st_all.at[f]), (cot_h, cot_all.at[f]), (w_h, w_all.at[z * 4 + x, c]), (probs_h, probs)])]
     for cp in local:
         cp.start()
-    pl.semaphore_wait(bar, 7 + 15 + 1 + 3 + 16 - own0.astype(jnp.int32) - own1.astype(jnp.int32))
+    pl.semaphore_wait(bar, 7 + 15 + 1 + 3 + 8 - (own0 & (pair == c)).astype(jnp.int32) - (own1 & (pair == c)).astype(jnp.int32))
 
     class Gather:
         def __init__(self, buf):
             other = (1 - h) * 4 + y
-            rows = [pl.ds(k * 256, 256) for k in range(2)]
-            self.first = [copy(buf.at[f, r], buf.at[f, r], at(dh=1)) for r in rows]
-            self.ring = [copy(buf.at[f], buf.at[f], at(dy=j)) for j in (1, 3, 2)]
-            self.fwd = [[copy(buf.at[other, r], buf.at[other, r], at(dy=j)) for j in (1, 3, 2)] for r in rows]
+            self.buf = buf
+            self.first = [self.piece(f, k, dict(dh=1)) for k in range(2)]
+            self.ring = [[self.piece(f, 0, dict(dy=1)), self.piece(f, 1, dict(dy=3))],
+                         [self.piece(f, 1, dict(dy=1)), self.piece(f, 0, dict(dy=3))]]
+            self.fwd = [[self.piece(other, k, dict(dy=1)), self.piece(other, k, dict(dy=3))] for k in range(2)]
+            self.hop = [[self.piece(e * 4 + (y + 3) % 4, 0, dict(dy=1)), self.piece(e * 4 + (y + 1) % 4, 1, dict(dy=3))]
+                        for e in (h, 1 - h)]
+
+        def piece(self, block, k, to):
+            ref = self.buf.at[block, pl.ds(k * 256, 256)]
+            return copy(ref, ref, at(**to))
 
         def begin_z(self):
             for cp in self.first:
                 start(cp)
 
         def begin_y(self):
-            for cp in self.ring:
+            for cp in self.ring[0] + self.ring[1]:
                 start(cp)
 
-        def middle(self):
-            for k in range(2):
-                self.first[k].wait_recv()
-                for cp in self.fwd[k]:
-                    start(cp)
-
-        def finish_a(self):
-            for cp in self.ring + self.fwd[0]:
+        def ring_fwd(self):
+            for i in range(2):
+                self.ring[0][i].wait_recv()
+                start(self.hop[0][i])
+
+        def middle(self, k):
+            self.first[k].wait_recv()
+            for cp in self.fwd[k]:
+                start(cp)
+
+        def tail_fwd(self):
+            self.fwd[0][0].wait_recv()
+            start(self.hop[1][0])
+            self.fwd[1][1].wait_recv()
+            start(self.hop[1][1])
+
+        def own_half(self):
+            for cp in self.ring[1] + self.hop[0]:
                 cp.wait_recv()
 
-        def finish_b(self):
-            for cp in self.fwd[1]:
+        def finish(self):
+            for cp in [self.fwd[0][1], self.fwd[1][0]] + self.hop[1]:
                 cp.wait_recv()
 
     g_st, g_cot, g_v = Gather(st_all), Gather(cot_all), Gather(v_all)
@@ -138,14 +156,17 @@
         keep_s[pl.ds(s * ORBS, ORBS), :] = jnp.where(forced, 0.0, 1.0)
     for cp in local[1:]:
         cp.wait()
-    g_st.middle()
+    g_st.ring_fwd()
+    g_st.middle(0)
+    g_st.middle(1)
     g_cot.begin_z()
     w_me = w_all.at[z * 4 + x, c]
     w_cps = [start(copy(w_me, w_me, at(dz=a, dx=b))) for a, b in dp_offs]
     w_core = copy(w_all.at[:, c], w_all.at[:, c], at(dc=1))
-    g_st.finish_a()
+    g_st.own_half()
+    g_st.tail_fwd()
     g_cot.begin_y()
-    g_st.finish_b()
+    g_st.finish()
 
     def norm(t, _):
         rows = pl.ds(pl.multiple_of(t * 32, 32), 32)
@@ -229,9 +250,11 @@
         ci = f * B + lax.broadcasted_iota(jnp.int32, (R, B), 1)
         t = t + jnp.where(ri == ci, damping, 0.0)
         nsrc[k - 1, 0] = total(t * t)
+        return None
+
+    def agz_start(k):
         for cp in agz_cp[k - 1] + nz_cp[k - 1]:
             start(cp)
-        return None
 
     def agz_done(k):
         gathered(k - 1, agz_cp[k - 1] + nz_cp[k - 1], 0, 0, 7)
@@ -287,36 +310,46 @@
     t_base = []
     for _ in range(2):
         t_base.append(count[0])
-        count[0] += 8
-    t_slot = (fd // 4) * 4 + d % 4
+        count[0] += 4
+    t_slot = (fd // 4) * 2 + pair
+    t_pair = [copy(tpo.at[0, 0], tp.at[0, 0, c], at(dc=1)),
+              copy(tpo.at[1], tp.at[1, :, c], at(dc=1))]
 
     def t_copy(i, e, m, slot):
         if i == 0:
-            dev = {"dp": 4 * f + m, "fac": e * 4 + fd % 4}
+            dev = {"dp": 4 * f + 2 * c + m, "fac": e * 4 + fd % 4}
         else:
-            dev = {"dp": 4 * (e * 4 + y) + m, "fac": h * 4 + fd % 4}
+            dev = {"dp": 4 * (e * 4 + y) + 2 * c + m, "fac": h * 4 + fd % 4}
         return pltpu.make_async_remote_copy(
-            src_ref=tsrc.at[i, 0 if i == 0 else e, m // 2], dst_ref=tdst.at[i, slot],
-            send_sem=ssem.at[t_base[i] + e * 4 + m], recv_sem=rsem.at[t_base[i] + slot],
+            src_ref=tsrc.at[i, 0 if i == 0 else e, m], dst_ref=tdst.at[i, slot],
+            send_sem=ssem.at[t_base[i] + e * 2 + m], recv_sem=rsem.at[t_base[i] + slot],
             device_id=dev, device_id_type=pl.DeviceIdType.MESH)
 
     def t_here(i, e, m):
         if i == 0:
-            return own0 & (d == 4 * f + m) & (h == e)
-        return own1 & (d == 4 * (e * 4 + y) + m)
-
-    def t_send(i, value):
-        for e in range(value.shape[1] // B):
-            for q in range(2):
-                tsrc[i, e, q] = value[:, e * B + q * 128:e * B + (q + 1) * 128]
+            return own0 & (d == 4 * f + 2 * c + m) & (h == e)
+        return own1 & (d == 4 * (e * 4 + y) + 2 * c + m)
+
+    def t_core(i, value):
+        for e in range(i + 1):
+            lo = value[:, e * B:e * B + 128]
+            hi = value[:, e * B + 128:(e + 1) * B]
+            tp[i, e, c] = jnp.where(c == 0, lo, hi)
+            tpo[i, e] = jnp.where(c == 0, hi, lo)
+        start(t_pair[i])
+
+    def t_send(i):
+        t_pair[i].wait_recv()
+        for e in range(i + 1):
+            tsrc[i, e] = tp[i, e].reshape(128, 128).T.reshape(2, R, 128)
         for e in range(2):
-            for m in range(4):
+            for m in range(2):
                 here = t_here(i, e, m)
 
                 @pl.when(here)
                 def _(e=e, m=m):
                     pltpu.make_async_copy(
-                        tsrc.at[i, 0 if i == 0 else e, m // 2], tdst.at[i, t_slot],
+                        tsrc.at[i, 0 if i == 0 else e, m], tdst.at[i, t_slot],
                         rsem.at[t_base[i] + t_slot]).start()
 
                 @pl.when(jnp.logical_not(here))
@@ -324,23 +357,24 @@
                     t_copy(i, e, m, t_slot).start()
 
     def t_recv(i):
-        for k in range(8):
-            t_copy(i, k // 4, k % 4, k).wait_recv()
-        for e in range(2):
-            s = jnp.concatenate([tdst[i, e * 4 + k] for k in range(4)], axis=0)
-            tt[:, e * B:(e + 1) * B] = s.T
-        return tt[pl.ds(pl.multiple_of((d % 2) * R, R), R), :]
+        for k in range(4):
+            t_copy(i, k // 2, k % 2, k).wait_recv()
+        return jnp.concatenate([tdst[i, k] for k in range(4)], axis=1)
 
     lax.fori_loop(0, TOK // 32, norm, 0)
     gram(1, n_all, n_all)
     start(core_cp[1])
-    g_cot.middle()
+    g_cot.ring_fwd()
+    core_done(1)
     for cp in w_cps:
         cp.wait_recv()
     start(w_core)
-    core_done(1)
-    g_cot.finish_a()
-    g_cot.finish_b()
+    g_cot.middle(0)
+    g_cot.middle(1)
+    g_cot.own_half()
+    g_cot.tail_fwd()
+    x_done(1)
+    g_cot.finish()
     w_core.wait_recv()
 
     acc[...] = jnp.zeros_like(acc)
@@ -361,48 +395,53 @@
     g_v.begin_y()
     gram(0, n_all, v_all)
     start(core_cp[0])
-    x_done(1)
+    z_done(1)
+    agz_start(1)
     core_done(0)
-    z_done(1)
-    g_v.middle()
+    g_v.ring_fwd()
+    g_v.middle(0)
+    g_v.middle(1)
     x_done(0)
+    g_v.own_half()
+    g_v.tail_fwd()
     agz_done(1)
-    g_v.finish_a()
-    g_v.finish_b()
+    grad = z_done(0)
+    t_core(0, grad)
+    gx[f] = grad.astype(bf16)
+    t_send(0)
+    g_v.finish()
     gram(2, v_all, v_all)
     start(core_cp[2])
-    grad = z_done(0)
-    t_send(0, grad)
-    gx[f] = grad.astype(bf16)
-    for cp in gx_cp + [grad_part]:
-        start(cp)
     core_done(2)
-    agx_done(1)
     x0 = t_recv(0)
     step_send(0, x0)
+    agx_done(1)
+    x_done(2)
     agc_done(1)
-    x_done(2)
     a_alpha = alpha_of(1)
     c1 = 4.0 * x0 - a_alpha * step_mul(0, 1)
     step_send(1, c1)
     z_done(2)
+    agz_start(2)
     c2 = 6.0 * x0 - a_alpha * step_mul(1, 1)
     step_send(2, c2)
     agz_done(2)
+    for cp in gx_cp + [grad_part]:
+        start(cp)
     c3 = 4.0 * x0 - a_alpha * step_mul(2, 1)
-    t_send(1, c3)
+    t_core(1, c3)
+    t_send(1)
     agx_done(2)
     l0 = t_recv(1)
     step_send(3, l0)
+    agc_done(2)
+    g_alpha = alpha_of(2)
+    c1 = 4.0 * l0 - g_alpha * step_mul(3, 2)
+    step_send(4, c1)
     for cp in gx_cp + [grad_part]:
         cp.wait_recv()
-    agc_done(2)
-    q0 = both(2, lambda b: gx[b])
-    g_alpha = alpha_of(2)
     grads = jnp.concatenate([grad2[0], grad2[1]], axis=1)
-    q0 = q0 + damping * grads
-    c1 = 4.0 * l0 - g_alpha * step_mul(3, 2)
-    step_send(4, c1)
+    q0 = both(2, lambda b: gx[b]) + damping * grads
     c2 = 6.0 * l0 - g_alpha * step_mul(4, 2)
     step_send(5, c2)
 
@@ -436,7 +475,7 @@
         cp.wait_send()
     for i in range(2):
         for e in range(2):
-            for m in range(4):
+            for m in range(2):
                 @pl.when(jnp.logical_not(t_here(i, e, m)))
                 def _(i=i, e=e, m=m):
                     t_copy(i, e, m, 0).wait_send()
@@ -471,8 +510,10 @@
             V((2, R, B), f32),
             V((8, R, B), bf16),
             V((2, 2, 2, R, 128), f32),
-            V((2, 8, R, 128), f32),
-            V((128, 2 * B), f32),
+            V((2, 2, R, 128), f32),
+            V((2, 2, 2, R, 128), f32),
+            V((2, 4, R, 128), f32),
+            V((R, 2 * B), f32),
             V((6, 4, 2, R, B), bf16),
             V((2, 4, 8, 128), f32),
             V((2, 14, 8, 128), f32),

time: 183 us -> 166 us (0.907)
  Pallas kernels: 182 us -> 164 us
    pallas_call x1, Pallas kernels: 182 us -> 164 us  [per_device(): pl.pallas_call(kernel, out_shape=jax.ShapeDtypeStruct((R, B), f32), in_sp...]
where the time goes in v3:
time: 166 us
  Pallas kernels  164 us (99%)
    pallas_call x1, Pallas kernels, per_device(): pl.pallas_call(kernel, out_shape=jax.ShapeDtypeStruct((R, B), f32), in_sp...  164 us

profile of v3, /device:TPU:1, one launch (start us, length us, event | category | flops | bytes accessed | tf_op | source)
XLA Modules:
  0.0 165.9 jit_solution(2746280400510691620)
XLA Ops:
  0.0 164.4 %shard_map.64 = f32[64,256]{1,0:T(8,128)} custom-call(s32[2,256]{1,0:T(2,128)} %occ.1, bf16[512,256]{1,0:T(8,128)(2,1)} %stream_h.1, f32[1,2048]{1,0:T(1,128)} %bitcast.3, bf16[2,2,256,256]{3,2,1,0:T(8,128)(2,1)} %probs_h.1, bf16[64,256]{1,0:T(8,128)(2,1)} %bitcast.2, bf16[512,256]{1,0:T(8,128)(2,1)} %cot_h.1), custom_call_target="tpu_custom_call" | custom-call | tf_op jit(solution)/shard_map/pallas_call | solution.py:489
  164.4 1.5 copy.8

commit v4 on v3

--- a/solution.py
+++ b/solution.py
@@ -29,7 +29,7 @@
 
 def kernel(occ, stream_h, gain, probs_h, w_h, cot_h, out,
            cot_all, st_all, n_all, v_all, w_all, probs, acc, keep_s,
-           part, rc_b, s1_b, rx_b, s2_b, rz_b, slab,
+           part, part_f, s1_f, s2_f, rc_b, s1_b, rx_b, s2_b, rz_b, slab, s2g, rzg,
            grad2, gx, tp, tpo, tsrc, tdst, tt, xg, nsrc, nbuf, fin, lsem, ssem, rsem):
     d = lax.axis_index("dp")
     f = lax.axis_index("fac")
@@ -90,7 +90,7 @@
                 greet({"dp": src_d, "fac": h * 4 + fd % 4})
 
     local = [pltpu.make_async_copy(a, b, lsem.at[i]) for i, (a, b) in enumerate([
-        (stream_h, st_all.at[f]), (cot_h, cot_all.at[f]), (w_h, w_all.at[z * 4 + x, c]), (probs_h, probs)])]
+        (stream_h, st_all.at[f]), (cot_h, cot_all.at[f]), (w_h, w_all.at[z, x, c]), (probs_h, probs)])]
     for cp in local:
         cp.start()
     pl.semaphore_wait(bar, 7 + 15 + 1 + 3 + 8 - (own0 & (pair == c)).astype(jnp.int32) - (own1 & (pair == c)).astype(jnp.int32))
@@ -156,16 +156,22 @@
         keep_s[pl.ds(s * ORBS, ORBS), :] = jnp.where(forced, 0.0, 1.0)
     for cp in local[1:]:
         cp.wait()
+    w_z = [copy(w_all.at[z, x, c], w_all.at[z, x, c], at(dz=j)) for j in (2, 1, 3)]
+    w_x = [copy(w_all.at[:, x, c], w_all.at[:, x, c], at(dx=j)) for j in (1, 3, 2)]
+    w_core = copy(w_all.at[:, :, c], w_all.at[:, :, c], at(dc=1))
+    for cp in w_z:
+        start(cp)
     g_st.ring_fwd()
     g_st.middle(0)
     g_st.middle(1)
     g_cot.begin_z()
-    w_me = w_all.at[z * 4 + x, c]
-    w_cps = [start(copy(w_me, w_me, at(dz=a, dx=b))) for a, b in dp_offs]
-    w_core = copy(w_all.at[:, c], w_all.at[:, c], at(dc=1))
-    g_st.own_half()
+    for cp in w_z:
+        cp.wait_recv()
+    for cp in w_x:
+        start(cp)
     g_st.tail_fwd()
     g_cot.begin_y()
+    g_st.own_half()
     g_st.finish()
 
     def norm(t, _):
@@ -184,38 +190,45 @@
         def body(b, _):
             p = dot_t(left[b], right[f]) * SCALE
             part[k, pl.ds(b * 2, 2)] = p.astype(bf16).reshape(2, 2, R, B)
+            if k == 0:
+                part_f[pl.ds(b * 2, 2)] = p.reshape(2, 2, R, B)
             return 0
         lax.fori_loop(0, 8, body, 0)
 
-    core_cp = [copy(part.at[k, :, 1 - c], rc_b.at[k], at(dc=1)) for k in range(3)]
-    x_cp = [[copy(s1_b.at[k, :, (x + j) % 4], rx_b.at[k, j - 1], at(dx=j)) for j in (1, 3, 2)] for k in range(3)]
+    core_cp = [copy(part.at[k, :, 1 - c], rc_b.at[k], at(dc=1)) for k in range(2)]
+    x_cp = [[copy(s1_b.at[k, :, (x + j) % 4], rx_b.at[k, j - 1], at(dx=j)) for j in (1, 3, 2)] for k in range(2)]
 
     def core_done(k):
         core_cp[k].wait_recv()
 
         def body(q, _):
-            s1_b[k, q] = (part[k, pl.ds(q * 4, 4), c].astype(f32)
-                          + rc_b[k, pl.ds(q * 4, 4)].astype(f32)).astype(bf16)
+            mine = part_f[pl.ds(q * 4, 4), c] if k == 0 else part[k, pl.ds(q * 4, 4), c].astype(f32)
+            t = mine + rc_b[k, pl.ds(q * 4, 4)].astype(f32)
+            s1_b[k, q] = t.astype(bf16)
+            if k == 0:
+                s1_f[q] = t
             return 0
         lax.fori_loop(0, 4, body, 0)
         for cp in x_cp[k]:
             start(cp)
 
-    z_cp = [[copy(s2_b.at[k, (z + j) % 4], rz_b.at[k, j - 1], at(dz=j)) for j in (2, 1, 3)] for k in range(3)]
+    z_cp = [[copy(s2_b.at[k, (z + j) % 4], rz_b.at[k, j - 1], at(dz=j)) for j in (2, 1, 3)] for k in range(2)]
 
     def x_done(k):
         for cp in x_cp[k]:
             cp.wait_recv()
-        t = s1_b[k, :, x].astype(f32)
+        t = s1_f[:, x] if k == 0 else s1_b[k, :, x].astype(f32)
         for j in range(3):
             t = t + rx_b[k, j].astype(f32)
         s2_b[k] = t.astype(bf16)
+        if k == 0:
+            s2_f[...] = t
         for cp in z_cp[k]:
             start(cp)
 
-    agz_cp = [[copy(slab.at[k, h, z, x, c], slab.at[k, h, z, x, c], at(dh=a, dz=b)) for a, b in z8_offs] for k in range(2)]
-    agx_cp = [[copy(slab.at[k, :, :, x, c], slab.at[k, :, :, x, c], at(dx=j)) for j in (1, 3, 2)] for k in range(2)]
-    agc_cp = [copy(slab.at[k, :, :, :, c], slab.at[k, :, :, :, c], at(dc=1)) for k in range(2)]
+    agz_cp = [copy(slab.at[0, h, z, x, c], slab.at[0, h, z, x, c], at(dh=a, dz=b)) for a, b in z8_offs]
+    agx_cp = [copy(slab.at[0, :, :, x, c], slab.at[0, :, :, x, c], at(dx=j)) for j in (1, 3, 2)]
+    agc_cp = copy(slab.at[0, :, :, :, c], slab.at[0, :, :, :, c], at(dc=1))
     nz_cp = [[copy(nsrc.at[k, 0], nbuf.at[k, i], at(dh=a, dz=b)) for i, (a, b) in enumerate(z8_offs)] for k in range(2)]
     nx_cp = [[copy(nsrc.at[k, 1], nbuf.at[k, 7 + i], at(dx=j)) for i, j in enumerate((1, 3, 2))] for k in range(2)]
     nc_cp = [[copy(nsrc.at[k, 2], nbuf.at[k, 10], at(dc=1))] for k in range(2)]
@@ -239,37 +252,132 @@
     def z_done(k):
         for cp in z_cp[k]:
             cp.wait_recv()
-        t = s2_b[k, z].astype(f32)
+        t = s2_f[z] if k == 0 else s2_b[k, z].astype(f32)
         for j in range(3):
             t = t + rz_b[k, j].astype(f32)
         if k == 0:
             grad2[h] = t
             return t
-        slab[k - 1, h, z, x, c] = t.astype(bf16)
+        slab[0, h, z, x, c] = t.astype(bf16).reshape(2, R // 2, B)
         ri = d * R + lax.broadcasted_iota(jnp.int32, (R, B), 0)
         ci = f * B + lax.broadcasted_iota(jnp.int32, (R, B), 1)
         t = t + jnp.where(ri == ci, damping, 0.0)
         nsrc[k - 1, 0] = total(t * t)
         return None
 
-    def agz_start(k):
-        for cp in agz_cp[k - 1] + nz_cp[k - 1]:
+    def agz_start():
+        for cp in agz_cp + nz_cp[0]:
             start(cp)
 
-    def agz_done(k):
-        gathered(k - 1, agz_cp[k - 1] + nz_cp[k - 1], 0, 0, 7)
-        for cp in agx_cp[k - 1] + nx_cp[k - 1]:
+    def agz_done():
+        gathered(0, agz_cp + nz_cp[0], 0, 0, 7)
+        for cp in agx_cp + nx_cp[0]:
             start(cp)
 
-    def agx_done(k):
-        gathered(k - 1, agx_cp[k - 1] + nx_cp[k - 1], 1, 7, 3)
-        for cp in [agc_cp[k - 1]] + nc_cp[k - 1]:
+    def agx_done():
+        gathered(0, agx_cp + nx_cp[0], 1, 7, 3)
+        for cp in [agc_cp] + nc_cp[0]:
             start(cp)
 
-    def agc_done(k):
-        gathered(k - 1, [agc_cp[k - 1]] + nc_cp[k - 1], 2, 10, 1)
-        for cp in ny_cp[k - 1]:
+    def agc_done():
+        gathered(0, [agc_cp] + nc_cp[0], 2, 10, 1)
+        for cp in ny_cp[0]:
             start(cp)
+
+    class Half:
+        def __init__(self, q):
+            self.q = q
+            hh = h if q == 0 else 1 - h
+            self.hh = hh
+            self.planes = pl.ds(2 * hh, 2)
+            rows = pl.ds(8 * hh, 8)
+            self.core = copy(part.at[2, rows, 1 - c], rc_b.at[2, rows], at(dc=1))
+            self.xs = [copy(s1_b.at[2, self.planes, (x + j) % 4], rx_b.at[2, j - 1, self.planes], at(dx=j)) for j in (1, 3, 2)]
+            self.zs = [copy(s2g.at[q, (z + j) % 4], rzg.at[q, j - 1], at(dz=j)) for j in (2, 1, 3)]
+            own_piece = slab.at[1, h, 2 * hh + z // 2, x, c, z % 2]
+            self.agz = [copy(own_piece, own_piece, at(dh=a, dz=b)) for a, b in z8_offs]
+            regions = [(e, 2 * e if q == 0 else 2 * (1 - e)) for e in range(2)]
+            self.agx = [copy(slab.at[1, e, r:r + 2, x, c], slab.at[1, e, r:r + 2, x, c], at(dx=j))
+                        for j in (1, 3, 2) for e, r in regions]
+            self.agc = [copy(slab.at[1, e, r:r + 2, :, c], slab.at[1, e, r:r + 2, :, c], at(dc=1)) for e, r in regions]
+
+        def gram(self):
+            def body(i, _):
+                b = self.hh * 4 + i
+                p = dot_t(v_all[b], v_all[f]) * SCALE
+                part[2, pl.ds(b * 2, 2)] = p.astype(bf16).reshape(2, 2, R, B)
+                return 0
+            lax.fori_loop(0, 4, body, 0)
+            start(self.core)
+
+        def core_done(self):
+            self.core.wait_recv()
+
+            def body(i, _):
+                q = 2 * self.hh + i
+                s1_b[2, q] = (part[2, pl.ds(q * 4, 4), c].astype(f32)
+                              + rc_b[2, pl.ds(q * 4, 4)].astype(f32)).astype(bf16)
+                return 0
+            lax.fori_loop(0, 2, body, 0)
+            for cp in self.xs:
+                start(cp)
+
+        def x_done(self):
+            for cp in self.xs:
+                cp.wait_recv()
+            t = s1_b[2, self.planes, x].astype(f32)
+            for j in range(3):
+                t = t + rx_b[2, j, self.planes].astype(f32)
+            s2g[self.q] = t.astype(bf16).reshape(4, R // 2, B)
+            for cp in self.zs:
+                start(cp)
+
+        def z_done(self):
+            for cp in self.zs:
+                cp.wait_recv()
+            t = s2g[self.q, z].astype(f32)
+            for j in range(3):
+                t = t + rzg[self.q, j].astype(f32)
+            slab[1, h, 2 * self.hh + z // 2, x, c, z % 2] = t.astype(bf16)
+            first = ((2 * self.hh + z // 2) * 8 + x * 2 + c) * R + (z % 2) * (R // 2)
+            ri = first + lax.broadcasted_iota(jnp.int32, (R // 2, B), 0)
+            ci = f * B + lax.broadcasted_iota(jnp.int32, (R // 2, B), 1)
+            t = t + jnp.where(ri == ci, damping, 0.0)
+            if self.q == 0:
+                nsrc[1, 0] = total(t * t)
+            else:
+                nsrc[1, 0] += total(t * t)
+            for cp in self.agz + (nz_cp[1] if self.q else []):
+                start(cp)
+
+        def agz_done(self):
+            if self.q:
+                gathered(1, self.agz + nz_cp[1], 0, 0, 7)
+            else:
+                for cp in self.agz:
+                    cp.wait_recv()
+            for cp in self.agx + (nx_cp[1] if self.q else []):
+                start(cp)
+
+        def agx_done(self):
+            if self.q:
+                gathered(1, self.agx + nx_cp[1], 1, 7, 3)
+            else:
+                for cp in self.agx:
+                    cp.wait_recv()
+            for cp in self.agc + (nc_cp[1] if self.q else []):
+                start(cp)
+
+        def agc_done(self):
+            if self.q:
+                gathered(1, self.agc + nc_cp[1], 2, 10, 1)
+                for cp in ny_cp[1]:
+                    start(cp)
+            else:
+                for cp in self.agc:
+                    cp.wait_recv()
+
+    ga, gb = Half(0), Half(1)
 
     def alpha_of(k):
         for cp in ny_cp[k - 1]:
@@ -341,7 +449,7 @@
     def t_send(i):
         t_pair[i].wait_recv()
         for e in range(i + 1):
-            tsrc[i, e] = tp[i, e].reshape(128, 128).T.reshape(2, R, 128)
+            tsrc[i, e] = tp[i, e].reshape(128, 128).T.astype(bf16).reshape(2, R, 128)
         for e in range(2):
             for m in range(2):
                 here = t_here(i, e, m)
@@ -359,14 +467,14 @@
     def t_recv(i):
         for k in range(4):
             t_copy(i, k // 2, k % 2, k).wait_recv()
-        return jnp.concatenate([tdst[i, k] for k in range(4)], axis=1)
+        return jnp.concatenate([tdst[i, k].astype(f32) for k in range(4)], axis=1)
 
     lax.fori_loop(0, TOK // 32, norm, 0)
     gram(1, n_all, n_all)
     start(core_cp[1])
     g_cot.ring_fwd()
     core_done(1)
-    for cp in w_cps:
+    for cp in w_x:
         cp.wait_recv()
     start(w_core)
     g_cot.middle(0)
@@ -380,7 +488,7 @@
     acc[...] = jnp.zeros_like(acc)
 
     def og(b, _):
-        w_blk = w_all[pl.ds(b * 2, 2)].reshape(B, B)
+        w_blk = w_all[b // 2, pl.ds((b % 2) * 2, 2)].reshape(B, B)
         acc[...] += dot(cot_all[b], w_blk)
         return 0
 
@@ -396,45 +504,50 @@
     gram(0, n_all, v_all)
     start(core_cp[0])
     z_done(1)
-    agz_start(1)
+    agz_start()
     core_done(0)
     g_v.ring_fwd()
     g_v.middle(0)
-    g_v.middle(1)
     x_done(0)
     g_v.own_half()
-    g_v.tail_fwd()
-    agz_done(1)
+    ga.gram()
+    g_v.middle(1)
+    ga.core_done()
+    agz_done()
     grad = z_done(0)
     t_core(0, grad)
     gx[f] = grad.astype(bf16)
+    g_v.tail_fwd()
     t_send(0)
+    ga.x_done()
     g_v.finish()
-    gram(2, v_all, v_all)
-    start(core_cp[2])
-    core_done(2)
+    gb.gram()
+    ga.z_done()
+    gb.core_done()
     x0 = t_recv(0)
     step_send(0, x0)
-    agx_done(1)
-    x_done(2)
-    agc_done(1)
+    agx_done()
+    gb.x_done()
+    agc_done()
     a_alpha = alpha_of(1)
     c1 = 4.0 * x0 - a_alpha * step_mul(0, 1)
     step_send(1, c1)
-    z_done(2)
-    agz_start(2)
+    gb.z_done()
+    ga.agz_done()
     c2 = 6.0 * x0 - a_alpha * step_mul(1, 1)
     step_send(2, c2)
-    agz_done(2)
+    gb.agz_done()
     for cp in gx_cp + [grad_part]:
         start(cp)
+    ga.agx_done()
     c3 = 4.0 * x0 - a_alpha * step_mul(2, 1)
     t_core(1, c3)
     t_send(1)
-    agx_done(2)
+    gb.agx_done()
+    ga.agc_done()
     l0 = t_recv(1)
     step_send(3, l0)
-    agc_done(2)
+    gb.agc_done()
     g_alpha = alpha_of(2)
     c1 = 4.0 * l0 - g_alpha * step_mul(3, 2)
     step_send(4, c1)
@@ -496,23 +609,28 @@
             V((8, TOK, B), bf16),
             V((8, TOK, B), bf16),
             V((8, TOK, B), bf16),
-            V((16, 2, R, B), bf16),
+            V((4, 4, 2, R, B), bf16),
             V((2, 2, ORBS, ORBS), bf16),
             V((TOK, B), f32),
             V((TOK, 1), f32),
             V((3, 16, 2, R, B), bf16),
+            V((16, 2, R, B), f32),
+            V((4, 4, R, B), f32),
+            V((4, R, B), f32),
             V((3, 16, R, B), bf16),
             V((3, 4, 4, R, B), bf16),
             V((3, 3, 4, R, B), bf16),
             V((3, 4, R, B), bf16),
             V((3, 3, R, B), bf16),
-            V((2, 2, 4, 4, 2, R, B), bf16),
+            V((2, 2, 4, 4, 2, 2, R // 2, B), bf16),
+            V((2, 4, R // 2, B), bf16),
+            V((2, 3, R // 2, B), bf16),
             V((2, R, B), f32),
             V((8, R, B), bf16),
             V((2, 2, 2, R, 128), f32),
             V((2, 2, R, 128), f32),
-            V((2, 2, 2, R, 128), f32),
-            V((2, 4, R, 128), f32),
+            V((2, 2, 2, R, 128), bf16),
+            V((2, 4, R, 128), bf16),
             V((R, 2 * B), f32),
             V((6, 4, 2, R, B), bf16),
             V((2, 4, 8, 128), f32),

time: 166 us -> 156 us (0.940)
  Pallas kernels: 164 us -> 154 us
    pallas_call x1, Pallas kernels: 164 us -> 154 us  [per_device(): pl.pallas_call(kernel, out_shape=jax.ShapeDtypeStruct((R, B), f32), in_sp...]
where the time goes in v4:
time: 156 us
  Pallas kernels  154 us (99%)
    pallas_call x1, Pallas kernels, per_device(): pl.pallas_call(kernel, out_shape=jax.ShapeDtypeStruct((R, B), f32), in_sp...  154 us

profile of v4, /device:TPU:1, one launch (start us, length us, event | category | flops | bytes accessed | tf_op | source)
XLA Modules:
  0.0 155.9 jit_solution(4991996073234812248)
XLA Ops:
  0.0 154.4 %shard_map.64 = f32[64,256]{1,0:T(8,128)} custom-call(s32[2,256]{1,0:T(2,128)} %occ.1, bf16[512,256]{1,0:T(8,128)(2,1)} %stream_h.1, f32[1,2048]{1,0:T(1,128)} %bitcast.3, bf16[2,2,256,256]{3,2,1,0:T(8,128)(2,1)} %probs_h.1, bf16[64,256]{1,0:T(8,128)(2,1)} %bitcast.2, bf16[512,256]{1,0:T(8,128)(2,1)} %cot_h.1), custom_call_target="tpu_custom_call" | custom-call | tf_op jit(solution)/shard_map/pallas_call | solution.py:602
  154.4 1.5 copy.8

commit v5 on v4

--- a/solution.py
+++ b/solution.py
@@ -74,6 +74,7 @@
     greet(at(dc=1))
     for j in (1, 2, 3):
         greet(at(dh=1, dz=j))
+        greet(at(dy=j, dc=1))
     own0 = fd == f
     own1 = fd % 4 == y
     pair = x % 2
@@ -93,7 +94,7 @@
         (stream_h, st_all.at[f]), (cot_h, cot_all.at[f]), (w_h, w_all.at[z, x, c]), (probs_h, probs)])]
     for cp in local:
         cp.start()
-    pl.semaphore_wait(bar, 7 + 15 + 1 + 3 + 8 - (own0 & (pair == c)).astype(jnp.int32) - (own1 & (pair == c)).astype(jnp.int32))
+    pl.semaphore_wait(bar, 7 + 15 + 1 + 3 + 3 + 8 - (own0 & (pair == c)).astype(jnp.int32) - (own1 & (pair == c)).astype(jnp.int32))
 
     class Gather:
         def __init__(self, buf):
@@ -442,14 +443,14 @@
         for e in range(i + 1):
             lo = value[:, e * B:e * B + 128]
             hi = value[:, e * B + 128:(e + 1) * B]
-            tp[i, e, c] = jnp.where(c == 0, lo, hi)
-            tpo[i, e] = jnp.where(c == 0, hi, lo)
+            tp[i, e, c] = jnp.where(c == 0, lo, hi).astype(bf16)
+            tpo[i, e] = jnp.where(c == 0, hi, lo).astype(bf16)
         start(t_pair[i])
 
     def t_send(i):
         t_pair[i].wait_recv()
         for e in range(i + 1):
-            tsrc[i, e] = tp[i, e].reshape(128, 128).T.astype(bf16).reshape(2, R, 128)
+            tsrc[i, e] = tp[i, e].astype(f32).reshape(128, 128).T.astype(bf16).reshape(2, R, 128)
         for e in range(2):
             for m in range(2):
                 here = t_here(i, e, m)
@@ -556,31 +557,28 @@
     grads = jnp.concatenate([grad2[0], grad2[1]], axis=1)
     q0 = both(2, lambda b: gx[b]) + damping * grads
     c2 = 6.0 * l0 - g_alpha * step_mul(4, 2)
+    fin[0] = total(4.0 * grads * l0 - g_alpha * (q0 * c2))
+    yc_offs = [(2, 0), (2, 1), (1, 0), (3, 0), (1, 1), (3, 1), (0, 1)]
+    fa = [copy(fin.at[0], fin.at[1 + i], at(dy=a, dc=b)) for i, (a, b) in enumerate(yc_offs)]
+    fx = [copy(fin.at[8], fin.at[9 + i], at(dz=a, dx=b)) for i, (a, b) in enumerate(dp_offs)]
+    for cp in fa:
+        start(cp)
     step_send(5, c2)
-
-    fin[0] = total(4.0 * grads * l0 - g_alpha * (q0 * c2))
-    fc = start(copy(fin.at[0], fin.at[1], at(dc=1)))
-    fx = [copy(fin.at[2], fin.at[3 + i], at(dz=a, dx=b)) for i, (a, b) in enumerate(dp_offs)]
-    fy = [copy(fin.at[18], fin.at[19 + i], at(dy=j)) for i, j in enumerate((2, 1, 3))]
-    fc.wait_recv()
-    fin[2] = fin[0] + fin[1]
+    for cp in fa:
+        cp.wait_recv()
+    t = fin[0]
+    for i in range(7):
+        t = t + fin[1 + i]
+    fin[8] = t
     for cp in fx:
         start(cp)
     c3 = 4.0 * l0 - g_alpha * step_mul(5, 2)
     ab = a_alpha * g_alpha
+    tt[0:R, :] = c3 * ab
     for cp in fx:
         cp.wait_recv()
-    t = fin[2]
     for i in range(15):
-        t = t + fin[3 + i]
-    fin[18] = t
-    for cp in fy:
-        start(cp)
-    tt[0:R, :] = c3 * ab
-    for cp in fy:
-        cp.wait_recv()
-    for i in range(3):
-        t = t + fin[19 + i]
+        t = t + fin[9 + i]
     inner = t[0:1, 0:1] * ab
     out[...] = tt[0:R, pl.ds(pl.multiple_of(h * B, B), B)] * (float(D) / jnp.sqrt(inner + epsilon))
 
@@ -627,15 +625,15 @@
             V((2, 3, R // 2, B), bf16),
             V((2, R, B), f32),
             V((8, R, B), bf16),
-            V((2, 2, 2, R, 128), f32),
-            V((2, 2, R, 128), f32),
+            V((2, 2, 2, R, 128), bf16),
+            V((2, 2, R, 128), bf16),
             V((2, 2, 2, R, 128), bf16),
             V((2, 4, R, 128), bf16),
             V((R, 2 * B), f32),
             V((6, 4, 2, R, B), bf16),
             V((2, 4, 8, 128), f32),
             V((2, 14, 8, 128), f32),
-            V((22, 8, 128), f32),
+            V((24, 8, 128), f32),
             pltpu.SemaphoreType.DMA((4,)),
             pltpu.SemaphoreType.DMA((NSEM,)),
             pltpu.SemaphoreType.DMA((NSEM,)),

time: 156 us -> 155 us (level)
  no operation moved by 1% of the time
where the time goes in v5:
time: 155 us
  Pallas kernels  154 us (99%)
    pallas_call x1, Pallas kernels, per_device(): pl.pallas_call(kernel, out_shape=jax.ShapeDtypeStruct((R, B), f32), in_sp...  154 us

profile of v5, /device:TPU:1, one launch (start us, length us, event | category | flops | bytes accessed | tf_op | source)
XLA Modules:
  0.0 155.2 jit_solution(6448372812105467787)
XLA Ops:
  0.0 153.7 %shard_map.64 = f32[64,256]{1,0:T(8,128)} custom-call(s32[2,256]{1,0:T(2,128)} %occ.1, bf16[512,256]{1,0:T(8,128)(2,1)} %stream_h.1, f32[1,2048]{1,0:T(1,128)} %bitcast.3, bf16[2,2,256,256]{3,2,1,0:T(8,128)(2,1)} %probs_h.1, bf16[64,256]{1,0:T(8,128)(2,1)} %bitcast.2, bf16[512,256]{1,0:T(8,128)(2,1)} %cot_h.1), custom_call_target="tpu_custom_call" | custom-call | tf_op jit(solution)/shard_map/pallas_call | solution.py:600
  153.7 1.5 copy.8

commit v6 on v5

--- a/solution.py
+++ b/solution.py
@@ -16,7 +16,7 @@
 epsilon = 1e-06
 bf16 = jnp.bfloat16
 f32 = jnp.float32
-NSEM = 240
+NSEM = 280
 
 
 def dot(a, b):
@@ -100,15 +100,16 @@
         def __init__(self, buf):
             other = (1 - h) * 4 + y
             self.buf = buf
-            self.first = [self.piece(f, k, dict(dh=1)) for k in range(2)]
+            self.first = [self.piece(f, k, dict(dh=1), 128) for k in range(4)]
             self.ring = [[self.piece(f, 0, dict(dy=1)), self.piece(f, 1, dict(dy=3))],
                          [self.piece(f, 1, dict(dy=1)), self.piece(f, 0, dict(dy=3))]]
-            self.fwd = [[self.piece(other, k, dict(dy=1)), self.piece(other, k, dict(dy=3))] for k in range(2)]
-            self.hop = [[self.piece(e * 4 + (y + 3) % 4, 0, dict(dy=1)), self.piece(e * 4 + (y + 1) % 4, 1, dict(dy=3))]
-                        for e in (h, 1 - h)]
-
-        def piece(self, block, k, to):
-            ref = self.buf.at[block, pl.ds(k * 256, 256)]
+            self.fwd = [[self.piece(other, k, dict(dy=1), 128), self.piece(other, k, dict(dy=3), 128)] for k in range(4)]
+            up, down = (y + 3) % 4, (y + 1) % 4
+            self.hop = [self.piece(h * 4 + up, 0, dict(dy=1)), self.piece(h * 4 + down, 1, dict(dy=3))]
+            self.far = [self.piece((1 - h) * 4 + (up if k < 2 else down), k, dict(dy=1 if k < 2 else 3), 128) for k in range(4)]
+
+        def piece(self, block, k, to, n=256):
+            ref = self.buf.at[block, pl.ds(k * n, n)]
             return copy(ref, ref, at(**to))
 
         def begin_z(self):
@@ -122,25 +123,27 @@
         def ring_fwd(self):
             for i in range(2):
                 self.ring[0][i].wait_recv()
-                start(self.hop[0][i])
-
-        def middle(self, k):
-            self.first[k].wait_recv()
-            for cp in self.fwd[k]:
-                start(cp)
+                start(self.hop[i])
+
+        def middle(self, half):
+            for k in (2 * half, 2 * half + 1):
+                self.first[k].wait_recv()
+                for cp in self.fwd[k]:
+                    start(cp)
 
         def tail_fwd(self):
-            self.fwd[0][0].wait_recv()
-            start(self.hop[1][0])
-            self.fwd[1][1].wait_recv()
-            start(self.hop[1][1])
+            for k in range(4):
+                self.fwd[k][k // 2].wait_recv()
+                start(self.far[k])
 
         def own_half(self):
-            for cp in self.ring[1] + self.hop[0]:
+            for cp in self.ring[1] + self.hop:
                 cp.wait_recv()
 
         def finish(self):
-            for cp in [self.fwd[0][1], self.fwd[1][0]] + self.hop[1]:
+            for k in range(4):
+                self.fwd[k][1 - k // 2].wait_recv()
+            for cp in self.far:
                 cp.wait_recv()
 
     g_st, g_cot, g_v = Gather(st_all), Gather(cot_all), Gather(v_all)

time: 155 us -> 155 us (level)
  no operation moved by 1% of the time
where the time goes in v6:
time: 155 us
  Pallas kernels  153 us (99%)
    pallas_call x1, Pallas kernels, per_device(): pl.pallas_call(kernel, out_shape=jax.ShapeDtypeStruct((R, B), f32), in_sp...  153 us

profile of v6, /device:TPU:1, one launch (start us, length us, event | category | flops | bytes accessed | tf_op | source)
XLA Modules:
  0.0 154.7 jit_solution(5048766550454680698)
XLA Ops:
  0.0 153.3 %shard_map.64 = f32[64,256]{1,0:T(8,128)} custom-call(s32[2,256]{1,0:T(2,128)} %occ.1, bf16[512,256]{1,0:T(8,128)(2,1)} %stream_h.1, f32[1,2048]{1,0:T(1,128)} %bitcast.3, bf16[2,2,256,256]{3,2,1,0:T(8,128)(2,1)} %probs_h.1, bf16[64,256]{1,0:T(8,128)(2,1)} %bitcast.2, bf16[512,256]{1,0:T(8,128)(2,1)} %cot_h.1), custom_call_target="tpu_custom_call" | custom-call | tf_op jit(solution)/shard_map/pallas_call | solution.py:603
  153.3 1.5 copy.8
